TPU v7x, 32 devices: a whole 2x2x4 slice. The times are simulated.
32 devices in a mesh: row: 8 (over z, x), col: 4 (over y, core).
Axes of the slice: x: 2, y: 2, z: 4, core: 2. Of those that a mesh axis runs over, the one named last changes fastest.
Arguments:
- object_slices: float32 [2, 4, 2048, 1024], P(None, None, 'row', 'col'), may hold values from -1 to 1
- positions: int32 [8, 4, 2, 2], P('row', 'col'), may hold values from 0 to 128
- intensities: float32 [8, 4, 2, 256, 256], P('row', 'col'), may hold values from 0 to 0.8
- probe: float32 [2, 256, 256], replicated, may hold values from -6 to 6
- propagator: float32 [256, 256], replicated, may hold values from -3.140625 to 3.140625
Outputs:
- gradient: float32 [2, 4, 2048, 1024], P(None, None, 'row', 'col')
- updated: float32 [2, 4, 2048, 1024], P(None, None, 'row', 'col')
Inputs may be any that keep to these rules, and one draw needn't show every extreme that they name: `positions`: each probe window lies inside its tile widened by 64 pixels on every side.
All inputs are finite; a program needn't handle non-finite values.
Results may differ from a plain program's by a relative error of at most 0.0003.
Values sent between devices are 32-bit elements; how exact they have to be, the bound alone decides.
A program may use at most 128 MiB of HBM per device.

v0:
```python
import jax
import jax.numpy as jnp
import numpy as np
from jax import lax
from jax.experimental import pallas as pl
from jax.experimental.pallas import tpu as pltpu
from jax.sharding import PartitionSpec as P

HALO = 64


descent_rate = 0.5


def passed_along(block, axis, distance):
    devices = range(lax.axis_size(axis))
    route = [((i - distance) % len(devices), i) for i in devices]
    return lax.ppermute(block, axis, route)


def split(value):
    high = value.astype(jnp.bfloat16)
    low = (value - high.astype(jnp.float32)).astype(jnp.bfloat16)
    return high, low


def half_tables(width):
    half = width // 2
    place = np.arange(half)
    found = []
    for odd in (0, 1):
        angle = 2.0 * np.pi * (np.outer(2 * place + odd, place) % width) / width
        re = np.cos(angle) / np.sqrt(width)
        im = -np.sin(angle) / np.sqrt(width)
        found.append(np.block([[re, -im], [im, re]]).astype(np.float32))
    even, odd = found
    order = np.eye(width, dtype=np.float32)[np.concatenate([2 * place, 2 * place + 1])]
    six = np.stack([even, odd, even.T, odd.T, order, order.T])
    high = six.astype(jnp.bfloat16)
    low = (six - high.astype(np.float32)).astype(jnp.bfloat16)
    return np.stack([high, low])


def dot_left(pair, value):
    high, low = split(value)
    matrix = jnp.concatenate([pair[0], pair[0], pair[1]], 1)
    return jnp.dot(matrix, jnp.concatenate([high, low, high], 0), preferred_element_type=jnp.float32)


def dot_right(value, pair):
    high, low = split(value)
    matrix = jnp.concatenate([pair[0], pair[0], pair[1]], 0)
    return jnp.dot(jnp.concatenate([high, low, high], 1), matrix, preferred_element_type=jnp.float32)


def cut(value, dim):
    half = value.shape[dim] // 2
    return (lax.slice_in_dim(value, 0, half, axis=dim), lax.slice_in_dim(value, half, 2 * half, axis=dim))


def joined(first, second, dim):
    return jnp.concatenate([first, second], dim)


def forward_axis(re, im, dim, dot, even_matrix, odd_matrix):
    r0, r1 = cut(re, dim)
    i0, i1 = cut(im, dim)
    even_re, even_im = cut(dot(joined(r0 + r1, i0 + i1, dim), even_matrix), dim)
    odd_re, odd_im = cut(dot(joined(r0 - r1, i0 - i1, dim), odd_matrix), dim)
    return joined(even_re, odd_re, dim), joined(even_im, odd_im, dim)


def inverse_axis(re, im, dim, dot, even_matrix, odd_matrix):
    r0, r1 = cut(re, dim)
    i0, i1 = cut(im, dim)
    p_re, p_im = cut(dot(joined(r0, i0, dim), even_matrix), dim)
    q_re, q_im = cut(dot(joined(r1, i1, dim), odd_matrix), dim)
    return joined(p_re + q_re, p_re - q_re, dim), joined(p_im + q_im, p_im - q_im, dim)


def left_dot(value, pair):
    return dot_left(pair, value)


def turned_over(value, width, source, target):
    parts = [lax.slice_in_dim(value, at, at + width, axis=source) for at in range(0, value.shape[source], width)]
    return jnp.concatenate(parts, target)


def forward(re, im, pairs):
    width = re.shape[0]
    re, im = forward_axis(re, im, 0, left_dot, pairs(0), pairs(1))
    re, im = (turned_over(v, width, 1, 0) for v in (re, im))
    return forward_axis(re, im, 1, dot_right, pairs(2), pairs(3))


def inverse(re, im, pairs):
    width = re.shape[1]
    re, im = inverse_axis(re, im, 1, dot_right, pairs(0), pairs(1))
    re, im = (turned_over(v, width, 0, 1) for v in (re, im))
    return inverse_axis(re, im, 0, left_dot, pairs(2), pairs(3))


def hop(fields, phase_re, phase_im, pairs):
    width = fields[0][0].shape[0]
    re, im = forward(*(jnp.concatenate([f[c] for f in fields], 1) for c in range(2)), pairs)
    re, im = complex_product(re, im, *(jnp.concatenate([p] * len(fields), 0) for p in (phase_re, phase_im)))
    re, im = inverse(re, im, pairs)
    spans = [slice(at, at + width) for at in range(0, re.shape[1], width)]
    return [(re[:, span], im[:, span]) for span in spans]


def by_parity(value, pairs):
    return dot_right(dot_left(pairs(4), value), pairs(5))


def complex_product(left_re, left_im, right_re, right_im):
    return (left_re * right_re - left_im * right_im, left_re * right_im + left_im * right_re)


def slid(whole, shift, axis, span):
    turned = pltpu.roll(whole, lax.rem(span - shift, span), axis)
    kept = lax.broadcasted_iota(jnp.int32, whole[:-1].shape, axis) < span - shift
    return jnp.where(kept, turned[:-1], turned[1:])


def spread(whole, shift, axis, span):
    turned = pltpu.roll(whole, lax.rem(shift, span), axis)
    zero = jnp.zeros_like(turned[:1])
    first = jnp.concatenate([zero, turned], 0)
    other = jnp.concatenate([turned, zero], 0)
    moved = lax.broadcasted_iota(jnp.int32, first.shape, axis) < shift
    return jnp.where(moved, first, other)


def row_place(oy, rows, width):
    base = jnp.minimum(oy - lax.rem(oy, 8), rows - width - 8)
    return pl.ds(pl.multiple_of(base, 8), width + 8), oy - base


def lane_place(ox, lanes=128):
    early = ox < HALO
    return jnp.where(early, 2, 0), jnp.where(early, ox + lanes - HALO, ox - HALO)


def swapped(value):
    return pltpu.roll(value, HALO, value.ndim - 1)


def lower_lanes(value):
    return lax.broadcasted_iota(jnp.int32, value.shape, value.ndim - 1) < HALO


def entry_kernel(measured, phase, tables, ordered, phases):
    def pairs(index):
        return tables[0, index], tables[1, index]

    for c in range(2):
        phases[c] = by_parity(phase[c], pairs)
    for k in range(measured.shape[0]):
        ordered[k] = by_parity(measured[k], pairs)


def step_kernel(
    offsets, core, edges, right, left, right_ends, left_ends, ordered, probe, phases, tables,
    out, out_edges, to_right, to_left, to_right_ends, to_left_ends,
    ext, total, windows, waves,
):
    count = ordered.shape[0]
    width = ordered.shape[-1]
    layers = core.shape[1]
    last = layers - 1
    tall = core.shape[2]
    wide = core.shape[3] // 128
    rounds = wide + 1
    whole = tall + 2 * HALO
    pieces = ((0, HALO, True, 0), (HALO, tall, False, 0), (HALO + tall, HALO, True, HALO))

    def pairs(index):
        return tables[0, index], tables[1, index]

    def gather(layer, carry):
        for start, size, is_edge, at in pieces:
            rows, own = pl.ds(start, size), pl.ds(at, size)
            for c in range(2):
                source = edges if is_edge else core
                for j in range(wide):
                    ext[c, layer, j, rows, :] = source[c, layer, own, pl.ds(j * 128, 128)]
            r = (right_ends if is_edge else right)[layer, own, :]
            l = (left_ends if is_edge else left)[layer, own, :]
            low = lower_lanes(r)
            ext[0, layer, wide, rows, :] = jnp.where(low, r, swapped(l))
            ext[1, layer, wide, rows, :] = jnp.where(low, swapped(r), l)
        return carry

    lax.fori_loop(0, layers, gather, 0)
    total[...] = jnp.zeros_like(total)
    for k in range(count):
        waves[k, 0] = probe[...]

    def cut_layer(k, layer):
        rows, shift = row_place(offsets[k, 0], whole, width)
        first, turn = lane_place(offsets[k, 1])
        for c in range(2):
            blocks = jnp.stack(
                [ext[c, layer, lax.rem(first + j, rounds), rows, :] for j in range(rounds)]
            )
            blocks = slid(blocks, turn, 2, 128)
            for j in range(wide):
                part = blocks[j].reshape((width + 8) // 8, 8, 128)
                windows[k, layer, c, :, j * 128 : j * 128 + 128] = slid(part, shift, 1, 8).reshape(width, 128)

    def leave(k, layer):
        return complex_product(
            waves[k, layer, 0], waves[k, layer, 1], windows[k, layer, 0], windows[k, layer, 1]
        )

    def onward(layer, carry):
        for k in range(count):
            cut_layer(k, layer)
        fields = [leave(k, layer) for k in range(count)]
        for k, (re, im) in enumerate(hop(fields, phases[0], phases[1], pairs)):
            waves[k, layer + 1, 0] = re
            waves[k, layer + 1, 1] = im
        return carry

    lax.fori_loop(0, last, onward, 0)

    def record(k, layer, back_re, back_im):
        wave_re, wave_im = waves[k, layer, 0], waves[k, layer, 1]
        rows, shift = row_place(offsets[k, 0], whole, width)
        first, turn = lane_place(offsets[k, 1])
        terms = (wave_re * back_re + wave_im * back_im, wave_re * back_im - wave_im * back_re)
        for c in range(2):
            blocks = jnp.stack([terms[c][:, j * 128 : j * 128 + 128] for j in range(wide)])
            blocks = spread(blocks, turn, 2, 128)
            for j in range(rounds):
                part = spread(blocks[j].reshape(width // 8, 8, 128), shift, 1, 8)
                total[c, layer, lax.rem(first + j, rounds), rows, :] += part.reshape(width + 8, 128)

    for k in range(count):
        cut_layer(k, last)
        far_re, far_im = forward(*leave(k, last), pairs)
        misfit = far_re * far_re + far_im * far_im - ordered[k]
        back_re, back_im = inverse(misfit * far_re, misfit * far_im, pairs)
        record(k, last, back_re, back_im)
        waves[k, last, 0] = back_re
        waves[k, last, 1] = back_im

    def backward(step, carry):
        layer = last - step
        fields = []
        for k in range(count):
            back_re, back_im = waves[k, layer, 0], waves[k, layer, 1]
            slab_re, slab_im = windows[k, layer, 0], windows[k, layer, 1]
            fields.append(complex_product(back_re, back_im, slab_re, -slab_im))
        for k, (re, im) in enumerate(hop(fields, phases[0], -phases[1], pairs)):
            record(k, layer - 1, re, im)
            waves[k, layer - 1, 0] = re
            waves[k, layer - 1, 1] = im
        return carry

    lax.fori_loop(0, last, backward, 0)

    def hand_out(layer, carry):
        for start, size, is_edge, at in pieces:
            rows, own = pl.ds(start, size), pl.ds(at, size)
            for c in range(2):
                target = out_edges if is_edge else out
                for j in range(wide):
                    target[c, layer, own, pl.ds(j * 128, 128)] = total[c, layer, j, rows, :]
            re, im = total[0, layer, wide, rows, :], total[1, layer, wide, rows, :]
            low = lower_lanes(re)
            (to_right_ends if is_edge else to_right)[layer, own, :] = jnp.where(low, re, swapped(im))
            (to_left_ends if is_edge else to_left)[layer, own, :] = jnp.where(low, swapped(re), im)
        return carry

    lax.fori_loop(0, layers, hand_out, 0)


def packed(cells):
    wide = cells.shape[-1]
    head = jnp.concatenate([cells[0, ..., :HALO], cells[1, ..., :HALO]], -1)
    tail = jnp.concatenate([cells[0, ..., wide - HALO :], cells[1, ..., wide - HALO :]], -1)
    return head, tail


def like(array):
    return jax.ShapeDtypeStruct(array.shape, array.dtype)


def absorb(parts, cells, from_left, from_right):
    wide = cells.shape[-1]
    l, r = from_left[...], from_right[...]
    low = lower_lanes(l)
    zero = jnp.zeros_like(l)
    added = (
        (jnp.where(low, l, zero), jnp.where(low, zero, swapped(r))),
        (jnp.where(low, swapped(l), zero), jnp.where(low, zero, r)),
    )
    for c in range(2):
        parts[c, :, :, 0:128] = cells[c, :, :, 0:128] + added[c][0]
        for at in range(128, wide - 128, 128):
            parts[c, :, :, at : at + 128] = cells[c, :, :, at : at + 128]
        parts[c, :, :, wide - 128 : wide] = cells[c, :, :, wide - 128 : wide] + added[c][1]


def edges_kernel(edges, from_left, from_right, up, down):
    size = edges.shape[2] // 2
    top, bottom = pl.ds(0, size), pl.ds(size, size)
    absorb(up, edges.at[:, :, top, :], from_left.at[:, top, :], from_right.at[:, top, :])
    absorb(down, edges.at[:, :, bottom, :], from_left.at[:, bottom, :], from_right.at[:, bottom, :])


def final_kernel(cells, from_left, from_right, from_above, from_below, objects, gradient, updated):
    tall = cells.shape[2]
    absorb(gradient, cells, from_left, from_right)
    gradient[:, :, 0:HALO, :] += from_above[...]
    gradient[:, :, tall - HALO : tall, :] += from_below[...]
    updated[...] = objects[...] - descent_rate * gradient[...]


def on_device(object_slices, positions, intensities, probe, propagator):
    measured = intensities[0, 0]
    count, width = measured.shape[0], measured.shape[-1]
    layers, tall, broad = object_slices.shape[1:]
    wide = broad // 128
    tables = jnp.asarray(half_tables(width))
    phase = jnp.stack([jnp.cos(propagator), jnp.sin(propagator)])
    ordered, phases = pl.pallas_call(
        entry_kernel,
        out_shape=[like(measured), like(phase)],
        in_specs=[pl.BlockSpec(memory_space=pltpu.VMEM)] * 3,
        out_specs=[pl.BlockSpec(memory_space=pltpu.VMEM)] * 2,
        cost_estimate=pl.CostEstimate(flops=2**30, bytes_accessed=2**22, transcendentals=0),
    )(measured, phase, tables)
    above = passed_along(object_slices[:, :, tall - HALO :], "row", 1)
    below = passed_along(object_slices[:, :, :HALO], "row", -1)
    head, tail = packed(object_slices)
    right = passed_along(head, "col", -1)
    left = passed_along(tail, "col", 1)
    edges = jnp.concatenate([above, below], 2)
    head, tail = packed(edges)
    right_ends = passed_along(head, "col", -1)
    left_ends = passed_along(tail, "col", 1)
    vmem = pl.BlockSpec(memory_space=pltpu.VMEM)
    limit = pltpu.CompilerParams(vmem_limit_bytes=58 * 2**20)
    cells, edges, to_right, to_left, to_right_ends, to_left_ends = pl.pallas_call(
        step_kernel,
        out_shape=[like(v) for v in (object_slices, edges, right, left, right_ends, left_ends)],
        in_specs=[pl.BlockSpec(memory_space=pltpu.SMEM)] + [vmem] * 10,
        out_specs=[vmem] * 6,
        scratch_shapes=[
            pltpu.VMEM((2, layers, wide + 1, tall + 2 * HALO, 128), jnp.float32),
            pltpu.VMEM((2, layers, wide + 1, tall + 2 * HALO, 128), jnp.float32),
            pltpu.VMEM((count, layers, 2, width, width), jnp.float32),
            pltpu.VMEM((count, layers, 2, width, width), jnp.float32),
        ],
        compiler_params=limit,
    )(
        positions[0, 0], object_slices, edges, right, left, right_ends, left_ends,
        ordered, probe, phases, tables,
    )
    left_ends = passed_along(to_right_ends, "col", 1)
    right_ends = passed_along(to_left_ends, "col", -1)
    left = passed_along(to_right, "col", 1)
    right = passed_along(to_left, "col", -1)
    up, down = pl.pallas_call(
        edges_kernel,
        out_shape=[like(above), like(below)],
        in_specs=[vmem] * 3,
        out_specs=[vmem] * 2,
        compiler_params=limit,
    )(edges, left_ends, right_ends)
    from_above = passed_along(down, "row", 1)
    from_below = passed_along(up, "row", -1)
    plane = pl.BlockSpec((2, 1, tall, broad), lambda layer: (0, layer, 0, 0))
    strip = pl.BlockSpec((1, tall, 128), lambda layer: (layer, 0, 0))
    border = pl.BlockSpec((2, 1, HALO, broad), lambda layer: (0, layer, 0, 0))
    return tuple(
        pl.pallas_call(
            final_kernel,
            grid=(layers,),
            out_shape=[like(cells), like(cells)],
            in_specs=[plane, strip, strip, border, border, plane],
            out_specs=[plane, plane],
            compiler_params=limit,
        )(cells, left, right, from_above, from_below, object_slices)
    )


def solution(mesh):
    return jax.shard_map(
        on_device,
        mesh=mesh,
        in_specs=(
            P(None, None, "row", "col"),
            P("row", "col", None, None),
            P("row", "col", None, None, None),
            P(),
            P(),
        ),
        out_specs=(P(None, None, "row", "col"), P(None, None, "row", "col")),
        check_vma=False,
    )
```

profile of v0, /device:TPU:0, one launch (start us, length us, event | category | flops | bytes accessed | tf_op | source)
XLA Modules:
  0.0 111.1 jit_solution(434427363219634772)
XLA Ops:
  0.6 1.4 %fusion = (f32[2,4,64,256]{3,2,1,0:T(8,128)S(1)}, f32[2,4,64,256]{3,2,1,0:T(8,128)S(1)}) fusion(f32[2,4,256,256]{3,2,1,0:T(8,128)} %objects.1), kind=kLoop, calls=%fused_computation.17 | loop fusion | bytes 2097152 | tf_op jit(solution)/shard_map/slice | solution.py:338
  2.1 6.1 %collective-permute-start.1 = (f32[2,4,64,256]{3,2,1,0:T(8,128)S(1)}, f32[2,4,64,256]{3,2,1,0:T(8,128)S(1)}, u32[]{:S(2)}, u32[]{:S(2)}) collective-permute-start(f32[2,4,64,256]{3,2,1,0:T(8,128)S(1)} %get-tuple-element.26), channel_id=1, source_target_pairs={{4,0},{8,4},{12,8},{16,12},{20,16},{24,20},{28,24},{0,28},{5,1},{9... | collective-permute-start | bytes 1572872 | tf_op jit(solution)/shard_map/ppermute | solution.py:18
  8.7 0.7 collective-permute-start.2
  9.7 18.7 %collective-permute-done = f32[2,4,64,256]{3,2,1,0:T(8,128)S(1)} collective-permute-done((f32[2,4,64,256]{3,2,1,0:T(8,128)S(1)}, f32[2,4,64,256]{3,2,1,0:T(8,128)S(1)}, u32[]{:S(2)}, u32[]{:S(2)}) %collective-permute-start) | collective-permute-done | bytes 524320 | tf_op jit(solution)/shard_map/ppermute | solution.py:18
  28.7 0.9 pad_maximum_fusion.3
  29.6 1.1 %collective-permute-start.4 = (f32[4,128,128]{2,1,0:T(8,128)}, f32[4,128,128]{2,1,0:T(8,128)S(1)}, u32[]{:S(2)}, u32[]{:S(2)}) collective-permute-start(f32[4,128,128]{2,1,0:T(8,128)} %pad_maximum_fusion.3), channel_id=1, source_target_pairs={{1,0},{2,1},{3,2},{0,3},{5,4},{6,5},{7,6},{4,7},{9,8},{10,9},{11,1... | collective-permute-start | bytes 786440 | tf_op jit(solution)/shard_map/ppermute | solution.py:18
  30.8 0.8 pad_maximum_fusion.4
  31.6 0.9 cosine_bitcast_fusion
  32.6 0.8 pad_maximum_fusion.2.phase
  33.4 3.8 %shard_map.77 = (f32[2,256,256]{2,1,0:T(8,128)}, f32[2,256,256]{2,1,0:T(8,128)}) custom-call(f32[2,256,256]{2,1,0:T(8,128)} %bitcast.23, f32[2,256,256]{2,1,0:T(8,128)} %pad_maximum_fusion.2.phase, bf16[2,6,256,256]{3,2,1,0:T(8,128)(2,1)} %constant.2.clone.tables), custom_call_target="tpu_custom_call" | custom-call | flops 1073741824 | bytes 4194304 | tf_op jit(solution)/shard_map/pallas_call | solution.py:330
  37.2 1.5 %collective-permute-done.5.left_ends = f32[4,128,128]{2,1,0:T(8,128)} collective-permute-done((f32[4,128,128]{2,1,0:T(8,128)}, f32[4,128,128]{2,1,0:T(8,128)}, u32[]{:S(2)}, u32[]{:S(2)}) %collective-permute-start.5) | collective-permute-done | bytes 262176 | tf_op jit(solution)/shard_map/ppermute | solution.py:18
  38.8 26.2 %shard_map.78 = (f32[2,4,256,256]{3,2,1,0:T(8,128)}, f32[2,4,128,256]{3,2,1,0:T(8,128)}, f32[4,256,128]{2,1,0:T(8,128)}, f32[4,256,128]{2,1,0:T(8,128)}, f32[4,128,128]{2,1,0:T(8,128)}, /*index=5*/f32[4,128,128]{2,1,0:T(8,128)}) custom-call(s32[2,2]{1,0:T(2,128)} %bitcast.22, f32[2,4,256,256]{3,2,1,0:T(8,128)} %objects.1, f32[2,4,128,256]{3,2,1,0:T(8,128)} %copy-done.1, ...), custom_call_target="tpu_custom_call" | custom-call | tf_op jit(solution)/shard_map/pallas_call | solution.py:348
  65.0 1.7 %collective-permute-start.9 = (f32[4,128,128]{2,1,0:T(8,128)}, f32[4,128,128]{2,1,0:T(8,128)S(1)}, u32[]{:S(2)}, u32[]{:S(2)}) collective-permute-start(f32[4,128,128]{2,1,0:T(8,128)} %get-tuple-element.19), channel_id=1, source_target_pairs={{1,0},{2,1},{3,2},{0,3},{5,4},{6,5},{7,6},{4,7},{9,8},{10,9},{11,1... | collective-permute-start | bytes 786440 | tf_op jit(solution)/shard_map/ppermute | solution.py:18
  66.7 1.7 %collective-permute-start.7 = (f32[4,256,128]{2,1,0:T(8,128)}, f32[4,256,128]{2,1,0:T(8,128)S(1)}, u32[]{:S(2)}, u32[]{:S(2)}) collective-permute-start(f32[4,256,128]{2,1,0:T(8,128)} %get-tuple-element.16), channel_id=1, source_target_pairs={{1,0},{2,1},{3,2},{0,3},{5,4},{6,5},{7,6},{4,7},{9,8},{10,9},{11,1... | collective-permute-start | bytes 1572872 | tf_op jit(solution)/shard_map/ppermute | solution.py:18
  68.5 3.7 %collective-permute-done.8.from_left = f32[4,128,128]{2,1,0:T(8,128)S(1)} collective-permute-done((f32[4,128,128]{2,1,0:T(8,128)}, f32[4,128,128]{2,1,0:T(8,128)S(1)}, u32[]{:S(2)}, u32[]{:S(2)}) %collective-permute-start.8) | collective-permute-done | bytes 262176 | tf_op jit(solution)/shard_map/ppermute | solution.py:18
  72.1 1.6 %collective-permute-done.9.from_right = f32[4,128,128]{2,1,0:T(8,128)S(1)} collective-permute-done((f32[4,128,128]{2,1,0:T(8,128)}, f32[4,128,128]{2,1,0:T(8,128)S(1)}, u32[]{:S(2)}, u32[]{:S(2)}) %collective-permute-start.9) | collective-permute-done | bytes 262176 | tf_op jit(solution)/shard_map/ppermute | solution.py:18
  74.4 2.5 %shard_map.79 = (f32[2,4,64,256]{3,2,1,0:T(8,128)}, f32[2,4,64,256]{3,2,1,0:T(8,128)}) custom-call(f32[2,4,128,256]{3,2,1,0:T(8,128)} %get-tuple-element.17.edges, f32[4,128,128]{2,1,0:T(8,128)} %copy-done.10, f32[4,128,128]{2,1,0:T(8,128)} %copy-done.11), custom_call_target="tpu_custom_call" | custom-call | tf_op jit(solution)/shard_map/pallas_call | solution.py:368
  76.9 2.3 %collective-permute-start.10 = (f32[2,4,64,256]{3,2,1,0:T(8,128)}, f32[2,4,64,256]{3,2,1,0:T(8,128)S(1)}, u32[]{:S(2)}, u32[]{:S(2)}) collective-permute-start(f32[2,4,64,256]{3,2,1,0:T(8,128)} %get-tuple-element.20), channel_id=1, source_target_pairs={{28,0},{0,4},{4,8},{8,12},{12,16},{16,20},{20,24},{24,28},{29,1},{... | collective-permute-start | bytes 1572872 | tf_op jit(solution)/shard_map/ppermute | solution.py:18
  79.2 2.4 %collective-permute-start.11 = (f32[2,4,64,256]{3,2,1,0:T(8,128)}, f32[2,4,64,256]{3,2,1,0:T(8,128)S(1)}, u32[]{:S(2)}, u32[]{:S(2)}) collective-permute-start(f32[2,4,64,256]{3,2,1,0:T(8,128)} %get-tuple-element.21), channel_id=1, source_target_pairs={{4,0},{8,4},{12,8},{16,12},{20,16},{24,20},{28,24},{0,28},{5,1},{9... | collective-permute-start | bytes 1572872 | tf_op jit(solution)/shard_map/ppermute | solution.py:18
  81.6 1.7 %collective-permute-done.6.from_left = f32[4,256,128]{2,1,0:T(8,128)S(1)} collective-permute-done((f32[4,256,128]{2,1,0:T(8,128)}, f32[4,256,128]{2,1,0:T(8,128)S(1)}, u32[]{:S(2)}, u32[]{:S(2)}) %collective-permute-start.6) | collective-permute-done | bytes 524320 | tf_op jit(solution)/shard_map/ppermute | solution.py:18
  84.0 18.1 %collective-permute-done.10.from_above = f32[2,4,64,256]{3,2,1,0:T(8,128)S(1)} collective-permute-done((f32[2,4,64,256]{3,2,1,0:T(8,128)}, f32[2,4,64,256]{3,2,1,0:T(8,128)S(1)}, u32[]{:S(2)}, u32[]{:S(2)}) %collective-permute-start.10) | collective-permute-done | bytes 524320 | tf_op jit(solution)/shard_map/ppermute | solution.py:18
  102.1 2.9 %collective-permute-done.11.from_below = f32[2,4,64,256]{3,2,1,0:T(8,128)S(1)} collective-permute-done((f32[2,4,64,256]{3,2,1,0:T(8,128)}, f32[2,4,64,256]{3,2,1,0:T(8,128)S(1)}, u32[]{:S(2)}, u32[]{:S(2)}) %collective-permute-start.11) | collective-permute-done | bytes 524320 | tf_op jit(solution)/shard_map/ppermute | solution.py:18
  105.0 0.8 copy-done.7
  105.8 5.3 %shard_map.80 = (f32[2,4,256,256]{3,2,1,0:T(8,128)}, f32[2,4,256,256]{3,2,1,0:T(8,128)}) custom-call(f32[2,4,256,256]{3,2,1,0:T(8,128)} %get-tuple-element.14.cells, f32[4,256,128]{2,1,0:T(8,128)} %copy-done.4, f32[4,256,128]{2,1,0:T(8,128)} %copy-done.5, f32[2,4,64,256]{3,2,1,0:T(8,128)} %copy-done.6, f32[2,4,64,256]{3,2,1,0:T(8,128)} %copy-done.7, ...), custom_call_target="tpu_custom_call" | custom-call | tf_op jit(solution)/shard_map/pallas_call | solution.py:381
  (39 shorter events, 2.5 us)
Async XLA Ops:
  0.6 7.5 %copy-start = (f32[2,4,256,256]{3,2,1,0:T(8,128)S(1)}, f32[2,4,256,256]{3,2,1,0:T(8,128)}, u32[]{:S(2)}) copy-start(f32[2,4,256,256]{3,2,1,0:T(8,128)} %objects.1) | copy-start | bytes 6291460
  2.1 26.4 %collective-permute-start.1 = (f32[2,4,64,256]{3,2,1,0:T(8,128)S(1)}, f32[2,4,64,256]{3,2,1,0:T(8,128)S(1)}, u32[]{:S(2)}, u32[]{:S(2)}) collective-permute-start(f32[2,4,64,256]{3,2,1,0:T(8,128)S(1)} %get-tuple-element.26), channel_id=1, source_target_pairs={{4,0},{8,4},{12,8},{16,12},{20,16},{24,20},{28,24},{0,28},{5,1},{9... | collective-permute-start | bytes 1572872 | tf_op jit(solution)/shard_map/ppermute | solution.py:18
  8.1 20.3 %collective-permute-start = (f32[2,4,64,256]{3,2,1,0:T(8,128)S(1)}, f32[2,4,64,256]{3,2,1,0:T(8,128)S(1)}, u32[]{:S(2)}, u32[]{:S(2)}) collective-permute-start(f32[2,4,64,256]{3,2,1,0:T(8,128)S(1)} %get-tuple-element.27), channel_id=1, source_target_pairs={{28,0},{0,4},{4,8},{8,12},{12,16},{16,20},{20,24},{24,28},{29,1},{... | collective-permute-start | bytes 1572872 | tf_op jit(solution)/shard_map/ppermute | solution.py:18
  8.7 28.5 %collective-permute-start.2 = (f32[4,256,128]{2,1,0:T(8,128)S(1)}, f32[4,256,128]{2,1,0:T(8,128)S(1)}, u32[]{:S(2)}, u32[]{:S(2)}) collective-permute-start(f32[4,256,128]{2,1,0:T(8,128)S(1)} %pad_maximum_fusion), channel_id=1, source_target_pairs={{1,0},{2,1},{3,2},{0,3},{5,4},{6,5},{7,6},{4,7},{9,8},{10,9},{11,1... | collective-permute-start | bytes 1572872 | tf_op jit(solution)/shard_map/ppermute | solution.py:18
  9.6 27.6 %collective-permute-start.3 = (f32[4,256,128]{2,1,0:T(8,128)S(1)}, f32[4,256,128]{2,1,0:T(8,128)S(1)}, u32[]{:S(2)}, u32[]{:S(2)}) collective-permute-start(f32[4,256,128]{2,1,0:T(8,128)S(1)} %pad_maximum_fusion.1), channel_id=1, source_target_pairs={{3,0},{0,1},{1,2},{2,3},{7,4},{4,5},{5,6},{6,7},{11,8},{8,9},{9,10... | collective-permute-start | bytes 1572872 | tf_op jit(solution)/shard_map/ppermute | solution.py:18
  28.5 4.1 %copy-start.1 = (f32[2,4,128,256]{3,2,1,0:T(8,128)}, f32[2,4,128,256]{3,2,1,0:T(8,128)S(1)}, u32[]{:S(2)}) copy-start(f32[2,4,128,256]{3,2,1,0:T(8,128)S(1)} %constant_dynamic-update-slice_fusion.edges) | copy-start | bytes 3145732
  28.5 3.1 %copy-start.8 = (f32[256,256]{1,0:T(8,128)S(1)}, f32[256,256]{1,0:T(8,128)}, u32[]{:S(2)}) copy-start(f32[256,256]{1,0:T(8,128)} %param.10) | copy-start | bytes 786436
  29.6 7.6 %collective-permute-start.4 = (f32[4,128,128]{2,1,0:T(8,128)}, f32[4,128,128]{2,1,0:T(8,128)S(1)}, u32[]{:S(2)}, u32[]{:S(2)}) collective-permute-start(f32[4,128,128]{2,1,0:T(8,128)} %pad_maximum_fusion.3), channel_id=1, source_target_pairs={{1,0},{2,1},{3,2},{0,3},{5,4},{6,5},{7,6},{4,7},{9,8},{10,9},{11,1... | collective-permute-start | bytes 786440 | tf_op jit(solution)/shard_map/ppermute | solution.py:18
  31.6 7.1 %collective-permute-start.5 = (f32[4,128,128]{2,1,0:T(8,128)}, f32[4,128,128]{2,1,0:T(8,128)}, u32[]{:S(2)}, u32[]{:S(2)}) collective-permute-start(f32[4,128,128]{2,1,0:T(8,128)} %pad_maximum_fusion.4), channel_id=1, source_target_pairs={{3,0},{0,1},{1,2},{2,3},{7,4},{4,5},{5,6},{6,7},{11,8},{8,9},{9,10... | collective-permute-start | bytes 786440 | tf_op jit(solution)/shard_map/ppermute | solution.py:18
  37.2 1.6 %copy-start.2 = (f32[4,256,128]{2,1,0:T(8,128)}, f32[4,256,128]{2,1,0:T(8,128)S(1)}, u32[]{:S(2)}) copy-start(f32[4,256,128]{2,1,0:T(8,128)S(1)} %collective-permute-done.2.right) | copy-start | bytes 1572868
  37.2 1.5 %copy-start.3 = (f32[4,256,128]{2,1,0:T(8,128)}, f32[4,256,128]{2,1,0:T(8,128)S(1)}, u32[]{:S(2)}) copy-start(f32[4,256,128]{2,1,0:T(8,128)S(1)} %collective-permute-done.3.left) | copy-start | bytes 1572868
  37.2 1.5 %copy-start.9 = (f32[4,128,128]{2,1,0:T(8,128)}, f32[4,128,128]{2,1,0:T(8,128)S(1)}, u32[]{:S(2)}) copy-start(f32[4,128,128]{2,1,0:T(8,128)S(1)} %collective-permute-done.4.right_ends) | copy-start | bytes 786436
  65.0 7.2 %collective-permute-start.8 = (f32[4,128,128]{2,1,0:T(8,128)}, f32[4,128,128]{2,1,0:T(8,128)S(1)}, u32[]{:S(2)}, u32[]{:S(2)}) collective-permute-start(f32[4,128,128]{2,1,0:T(8,128)} %get-tuple-element.18), channel_id=1, source_target_pairs={{3,0},{0,1},{1,2},{2,3},{7,4},{4,5},{5,6},{6,7},{11,8},{8,9},{9,10... | collective-permute-start | bytes 786440 | tf_op jit(solution)/shard_map/ppermute | solution.py:18
  65.0 8.8 %collective-permute-start.9 = (f32[4,128,128]{2,1,0:T(8,128)}, f32[4,128,128]{2,1,0:T(8,128)S(1)}, u32[]{:S(2)}, u32[]{:S(2)}) collective-permute-start(f32[4,128,128]{2,1,0:T(8,128)} %get-tuple-element.19), channel_id=1, source_target_pairs={{1,0},{2,1},{3,2},{0,3},{5,4},{6,5},{7,6},{4,7},{9,8},{10,9},{11,1... | collective-permute-start | bytes 786440 | tf_op jit(solution)/shard_map/ppermute | solution.py:18
  66.7 16.6 %collective-permute-start.6 = (f32[4,256,128]{2,1,0:T(8,128)}, f32[4,256,128]{2,1,0:T(8,128)S(1)}, u32[]{:S(2)}, u32[]{:S(2)}) collective-permute-start(f32[4,256,128]{2,1,0:T(8,128)} %get-tuple-element.15), channel_id=1, source_target_pairs={{3,0},{0,1},{1,2},{2,3},{7,4},{4,5},{5,6},{6,7},{11,8},{8,9},{9,10... | collective-permute-start | bytes 1572872 | tf_op jit(solution)/shard_map/ppermute | solution.py:18
  66.7 17.3 %collective-permute-start.7 = (f32[4,256,128]{2,1,0:T(8,128)}, f32[4,256,128]{2,1,0:T(8,128)S(1)}, u32[]{:S(2)}, u32[]{:S(2)}) collective-permute-start(f32[4,256,128]{2,1,0:T(8,128)} %get-tuple-element.16), channel_id=1, source_target_pairs={{1,0},{2,1},{3,2},{0,3},{5,4},{6,5},{7,6},{4,7},{9,8},{10,9},{11,1... | collective-permute-start | bytes 1572872 | tf_op jit(solution)/shard_map/ppermute | solution.py:18
  72.1 1.6 %copy-start.10 = (f32[4,128,128]{2,1,0:T(8,128)}, f32[4,128,128]{2,1,0:T(8,128)S(1)}, u32[]{:S(2)}) copy-start(f32[4,128,128]{2,1,0:T(8,128)S(1)} %collective-permute-done.8.from_left) | copy-start | bytes 786436
  73.7 0.7 copy-start.11
  76.9 25.2 %collective-permute-start.10 = (f32[2,4,64,256]{3,2,1,0:T(8,128)}, f32[2,4,64,256]{3,2,1,0:T(8,128)S(1)}, u32[]{:S(2)}, u32[]{:S(2)}) collective-permute-start(f32[2,4,64,256]{3,2,1,0:T(8,128)} %get-tuple-element.20), channel_id=1, source_target_pairs={{28,0},{0,4},{4,8},{8,12},{12,16},{16,20},{20,24},{24,28},{29,1},{... | collective-permute-start | bytes 1572872 | tf_op jit(solution)/shard_map/ppermute | solution.py:18
  79.2 25.8 %collective-permute-start.11 = (f32[2,4,64,256]{3,2,1,0:T(8,128)}, f32[2,4,64,256]{3,2,1,0:T(8,128)S(1)}, u32[]{:S(2)}, u32[]{:S(2)}) collective-permute-start(f32[2,4,64,256]{3,2,1,0:T(8,128)} %get-tuple-element.21), channel_id=1, source_target_pairs={{4,0},{8,4},{12,8},{16,12},{20,16},{24,20},{28,24},{0,28},{5,1},{9... | collective-permute-start | bytes 1572872 | tf_op jit(solution)/shard_map/ppermute | solution.py:18
  83.4 21.7 %copy-start.4 = (f32[4,256,128]{2,1,0:T(8,128)}, f32[4,256,128]{2,1,0:T(8,128)S(1)}, u32[]{:S(2)}) copy-start(f32[4,256,128]{2,1,0:T(8,128)S(1)} %collective-permute-done.6.from_left) | copy-start | bytes 1572868
  84.0 21.0 %copy-start.5 = (f32[4,256,128]{2,1,0:T(8,128)}, f32[4,256,128]{2,1,0:T(8,128)S(1)}, u32[]{:S(2)}) copy-start(f32[4,256,128]{2,1,0:T(8,128)S(1)} %collective-permute-done.7.from_right) | copy-start | bytes 1572868
  102.1 2.9 %copy-start.6 = (f32[2,4,64,256]{3,2,1,0:T(8,128)}, f32[2,4,64,256]{3,2,1,0:T(8,128)S(1)}, u32[]{:S(2)}) copy-start(f32[2,4,64,256]{3,2,1,0:T(8,128)S(1)} %collective-permute-done.10.from_above) | copy-start | bytes 1572868
  105.0 0.8 copy-start.7
where the time goes:
time: 111 us
  waiting for transfers between devices  48.9 us (44%)
  Pallas kernels  37.7 us (34%)
  starting transfers between devices  16.2 us (15%)
  local copies, waits for them, and re-layouts  4.54 us (4%)
  other arithmetic  2.98 us (3%)
    ppermute x12, waiting for transfers between devices, passed_along(): return lax.ppermute(block, axis, route)  48.9 us
    pallas_call x1, Pallas kernels, on_device(): pl.pallas_call(step_kernel, out_shape=[like(v) for v in (object_slices, e...  26.2 us
    ppermute x12, starting transfers between devices, passed_along(): return lax.ppermute(block, axis, route)  16.2 us
    pallas_call x1, Pallas kernels, on_device(): pl.pallas_call(final_kernel, grid=(layers,), out_shape=[like(cells), like...  5.29 us
    pallas_call x1, Pallas kernels, on_device(): pl.pallas_call(entry_kernel, out_shape=[like(measured), like(phase)], in_...  3.78 us
    pallas_call x1, Pallas kernels, on_device(): pl.pallas_call(edges_kernel, out_shape=[like(above), like(below)], in_spe...  2.47 us
  transfers between devices with their start and end apart: 12, of which 8 were waited for; matrix products, arithmetic and copies ran while one was open for 4% of the time, Pallas kernels for 6%

commit v1 on v0

v1 whole, which is shorter than its diff:
```python
import functools

import jax
import jax.numpy as jnp
import numpy as np
from jax import lax
from jax.experimental import pallas as pl
from jax.experimental.pallas import tpu as pltpu
from jax.sharding import PartitionSpec as P

HALO = 64
LANES = 128

descent_rate = 0.5


def split(value):
    high = value.astype(jnp.bfloat16)
    low = (value - high.astype(jnp.float32)).astype(jnp.bfloat16)
    return high, low


def half_tables(width):
    half = width // 2
    place = np.arange(half)
    found = []
    for odd in (0, 1):
        angle = 2.0 * np.pi * (np.outer(2 * place + odd, place) % width) / width
        re = np.cos(angle) / np.sqrt(width)
        im = -np.sin(angle) / np.sqrt(width)
        found.append(np.block([[re, -im], [im, re]]).astype(np.float32))
    even, odd = found
    order = np.eye(width, dtype=np.float32)[np.concatenate([2 * place, 2 * place + 1])]
    six = np.stack([even, odd, even.T, odd.T, order, order.T])
    high = six.astype(jnp.bfloat16)
    low = (six - high.astype(np.float32)).astype(jnp.bfloat16)
    return np.stack([high, low])


def dot_left(pair, value):
    high, low = split(value)
    matrix = jnp.concatenate([pair[0], pair[0], pair[1]], 1)
    return jnp.dot(matrix, jnp.concatenate([high, low, high], 0), preferred_element_type=jnp.float32)


def dot_right(value, pair):
    high, low = split(value)
    matrix = jnp.concatenate([pair[0], pair[0], pair[1]], 0)
    return jnp.dot(jnp.concatenate([high, low, high], 1), matrix, preferred_element_type=jnp.float32)


def cut(value, dim):
    half = value.shape[dim] // 2
    return (lax.slice_in_dim(value, 0, half, axis=dim), lax.slice_in_dim(value, half, 2 * half, axis=dim))


def joined(first, second, dim):
    return jnp.concatenate([first, second], dim)


def forward_axis(re, im, dim, dot, even_matrix, odd_matrix):
    r0, r1 = cut(re, dim)
    i0, i1 = cut(im, dim)
    even_re, even_im = cut(dot(joined(r0 + r1, i0 + i1, dim), even_matrix), dim)
    odd_re, odd_im = cut(dot(joined(r0 - r1, i0 - i1, dim), odd_matrix), dim)
    return joined(even_re, odd_re, dim), joined(even_im, odd_im, dim)


def inverse_axis(re, im, dim, dot, even_matrix, odd_matrix):
    r0, r1 = cut(re, dim)
    i0, i1 = cut(im, dim)
    p_re, p_im = cut(dot(joined(r0, i0, dim), even_matrix), dim)
    q_re, q_im = cut(dot(joined(r1, i1, dim), odd_matrix), dim)
    return joined(p_re + q_re, p_re - q_re, dim), joined(p_im + q_im, p_im - q_im, dim)


def left_dot(value, pair):
    return dot_left(pair, value)


def turned_over(value, width, source, target):
    parts = [lax.slice_in_dim(value, at, at + width, axis=source) for at in range(0, value.shape[source], width)]
    return jnp.concatenate(parts, target)


def forward(re, im, pairs):
    width = re.shape[0]
    re, im = forward_axis(re, im, 0, left_dot, pairs(0), pairs(1))
    re, im = (turned_over(v, width, 1, 0) for v in (re, im))
    return forward_axis(re, im, 1, dot_right, pairs(2), pairs(3))


def inverse(re, im, pairs):
    width = re.shape[1]
    re, im = inverse_axis(re, im, 1, dot_right, pairs(0), pairs(1))
    re, im = (turned_over(v, width, 0, 1) for v in (re, im))
    return inverse_axis(re, im, 0, left_dot, pairs(2), pairs(3))


def hop(fields, phase_re, phase_im, pairs):
    width = fields[0][0].shape[0]
    re, im = forward(*(jnp.concatenate([f[c] for f in fields], 1) for c in range(2)), pairs)
    re, im = complex_product(re, im, *(jnp.concatenate([p] * len(fields), 0) for p in (phase_re, phase_im)))
    re, im = inverse(re, im, pairs)
    spans = [slice(at, at + width) for at in range(0, re.shape[1], width)]
    return [(re[:, span], im[:, span]) for span in spans]


def by_parity(value, left, right):
    rows = jnp.dot(
        jnp.concatenate([left, left], 1), jnp.concatenate(split(value), 0), preferred_element_type=jnp.float32
    )
    return jnp.dot(
        jnp.concatenate(split(rows), 1), jnp.concatenate([right, right], 0), preferred_element_type=jnp.float32
    )


def complex_product(left_re, left_im, right_re, right_im):
    return (left_re * right_re - left_im * right_im, left_re * right_im + left_im * right_re)


def slid(whole, shift, axis, span):
    turned = pltpu.roll(whole, lax.rem(span - shift, span), axis)
    kept = lax.broadcasted_iota(jnp.int32, whole[:-1].shape, axis) < span - shift
    return jnp.where(kept, turned[:-1], turned[1:])


def spread(whole, shift, axis, span):
    turned = pltpu.roll(whole, lax.rem(shift, span), axis)
    zero = jnp.zeros_like(turned[:1])
    first = jnp.concatenate([zero, turned], 0)
    other = jnp.concatenate([turned, zero], 0)
    moved = lax.broadcasted_iota(jnp.int32, first.shape, axis) < shift
    return jnp.where(moved, first, other)


def row_place(oy, rows, width):
    base = jnp.minimum(lax.div(oy, 8), (rows - width) // 8 - 1)
    return base, oy - 8 * base


def lane_place(ox):
    early = ox < HALO
    return jnp.where(early, 2, 0), jnp.where(early, ox + LANES - HALO, ox - HALO)


def swapped(value):
    return pltpu.roll(value, HALO, value.ndim - 1)


def choose(low, high):
    lower = lax.broadcasted_iota(jnp.int32, low.shape, low.ndim - 1) < HALO
    return jnp.where(lower, low, high)


def ends_of(cells):
    (re0, re1), (im0, im1) = cells
    return choose(re0, swapped(im0)), choose(swapped(re1), im1)


def middle_of(cells):
    return [choose(swapped(first), swapped(second)) for first, second in cells]


def unpacked(head, tail, middle_re, middle_im):
    mid_re, mid_im = swapped(middle_re), swapped(middle_im)
    return (
        (choose(head, mid_re), choose(mid_re, swapped(tail))),
        (choose(swapped(head), mid_im), choose(mid_im, tail)),
    )


def step_kernel(
    offsets, objects, intensities, probe, propagator, tables_in,
    gradient, updated,
    tables, cells, measured, ordered, phase, phases, waves, windows, slab, spans, total,
    row_out, row_in, col_out, col_in, corner_in,
    grow_out, grow_in, gcol_out, gcol_in, gcorner_out, gcorner_in,
    load_sem, slice_sem, store_sem, row_sem, col_sem, corner_sem, grow_sem, gcol_sem, gcorner_sem,
):
    count, width = measured.shape[0], measured.shape[-1]
    layers, tall = cells.shape[1:3]
    last = layers - 1
    wide = cells.shape[3] // LANES
    rounds = wide + 1
    whole = tall + 2 * HALO
    pad = 2 * HALO

    rows_n, cols_n = lax.axis_size("row"), lax.axis_size("col")
    row, col = lax.axis_index("row"), lax.axis_index("col")
    below, above = lax.rem(row + 1, rows_n), lax.rem(row + rows_n - 1, rows_n)
    right, left = lax.rem(col + 1, cols_n), lax.rem(col + cols_n - 1, cols_n)
    row_to = ((below, col), (above, col))
    col_to = ((row, right), (row, left))

    def send(src, dst, sems, where, target):
        return pltpu.make_async_remote_copy(
            src_ref=src, dst_ref=dst, send_sem=sems.at[(0, *where)], recv_sem=sems.at[(1, *where)],
            device_id=target, device_id_type=pl.DeviceIdType.MESH,
        )

    def row_copy(layer, half, d):
        where = (layer, half, slice(None), d)
        return send(row_out.at[where], row_in.at[where], row_sem, (layer, half, d), row_to[d])

    def col_copy(layer, side):
        return send(col_out.at[layer, side], col_in.at[layer, side], col_sem, (layer, side), col_to[side])

    def corner_copy(layer, side):
        source = row_in.at[layer, 0, 1 - side]
        return send(source, corner_in.at[layer, side], corner_sem, (layer, side), col_to[side])

    def grow_copy(layer, half, d):
        where = (layer, half, slice(None), d)
        return send(grow_out.at[where], grow_in.at[where], grow_sem, (layer, half, d), row_to[d])

    def gcol_copy(layer, side):
        return send(gcol_out.at[layer, side], gcol_in.at[layer, side], gcol_sem, (layer, side), col_to[side])

    def gcorner_copy(layer, side):
        return send(
            gcorner_out.at[layer, side], gcorner_in.at[layer, side], gcorner_sem, (layer, side), col_to[side]
        )

    loads = [
        pltpu.make_async_copy(propagator, phase, load_sem.at[0]),
        pltpu.make_async_copy(tables_in, tables, load_sem.at[1]),
        pltpu.make_async_copy(intensities, measured, load_sem.at[2]),
    ] + [pltpu.make_async_copy(probe, waves.at[k, 0], load_sem.at[3 + k]) for k in range(count)]

    def slice_load(layer):
        return pltpu.make_async_copy(objects.at[:, layer], cells.at[:, layer], slice_sem.at[layer])

    barrier = pltpu.get_barrier_semaphore()
    for target in row_to + col_to:
        pl.semaphore_signal(barrier, inc=1, device_id=target, device_id_type=pl.DeviceIdType.MESH)
    for layer in range(layers):
        slice_load(layer).start()
    for load in loads:
        load.start()

    def lane_blocks(ref, layer, rows):
        return [[ref[c, layer, rows, pl.ds(j * LANES, LANES)] for j in range(wide)] for c in range(2)]

    def pack(layer, carry):
        slice_load(layer).wait()
        for d, at in enumerate((tall - HALO, 0)):
            strip = lane_blocks(cells, layer, pl.ds(at, HALO))
            for half, packs in enumerate((ends_of(strip), middle_of(strip))):
                for i in range(2):
                    row_out[layer, half, i, d] = packs[i]
        head, tail = ends_of(lane_blocks(cells, layer, pl.ds(0, tall)))
        col_out[layer, 0] = tail
        col_out[layer, 1] = head
        return carry

    lax.fori_loop(0, layers, pack, 0)
    pl.semaphore_wait(barrier, 4)

    def launch(layer, carry):
        for half in range(2):
            for d in range(2):
                row_copy(layer, half, d).start()
        for side in range(2):
            col_copy(layer, side).start()
        return carry

    lax.fori_loop(0, layers, launch, 0)

    def pairs(index):
        return tables[0, index], tables[1, index]

    for load in loads:
        load.wait()
    angle = phase[...]
    phases[0] = by_parity(jnp.cos(angle), tables[0, 4], tables[0, 5])
    phases[1] = by_parity(jnp.sin(angle), tables[0, 4], tables[0, 5])
    for k in range(count):
        ordered[k] = by_parity(measured[k], tables[0, 4], tables[0, 5])
    blank = jnp.zeros((pad // 8, 8, LANES), jnp.float32)
    for k in range(count):
        for c in range(2):
            for j in range(rounds):
                spans[k, c, j, pl.ds(0, pad // 8)] = blank
                spans[k, c, j, pl.ds((pad + width) // 8 + 1, pad // 8)] = blank

    pieces = ((0, HALO, 0), (HALO, tall, None), (HALO + tall, HALO, 1))

    def forward_corners(layer):
        for d in range(2):
            row_copy(layer, 0, d).wait_recv()
        for side in range(2):
            corner_copy(layer, side).start()

    def assemble(layer):
        for d in range(2):
            row_copy(layer, 1, d).wait_recv()
        for side in range(2):
            col_copy(layer, side).wait_recv()
            corner_copy(layer, side).wait_recv()
        for start, size, d in pieces:
            rows, tiles = pl.ds(start // 8, size // 8), (size // 8, 8, LANES)
            if d is None:
                blocks = lane_blocks(cells, layer, pl.ds(0, tall))
                l, r = col_in[layer, 0], col_in[layer, 1]
            else:
                blocks = unpacked(*(row_in[layer, half, i, d] for half in range(2) for i in range(2)))
                l, r = corner_in[layer, 0, d], corner_in[layer, 1, d]
            for c in range(2):
                for j in range(wide):
                    slab[c, j, rows] = blocks[c][j].reshape(tiles)
            slab[0, wide, rows] = choose(r, swapped(l)).reshape(tiles)
            slab[1, wide, rows] = choose(swapped(r), l).reshape(tiles)

    def cut_layer(k, layer):
        base, shift = row_place(offsets[0, 0, k, 0], whole, width)
        first, turn = lane_place(offsets[0, 0, k, 1])
        for c in range(2):
            blocks = jnp.stack(
                [slab[c, lax.rem(first + j, rounds), pl.ds(base, width // 8 + 1)] for j in range(rounds)]
            )
            blocks = slid(blocks, turn, 3, LANES)
            for j in range(wide):
                part = slid(blocks[j], shift, 1, 8)
                windows[k, layer, c, :, j * LANES : j * LANES + LANES] = part.reshape(width, LANES)

    def leave(k, layer):
        return complex_product(
            waves[k, layer, 0], waves[k, layer, 1], windows[k, layer, 0], windows[k, layer, 1]
        )

    def onward(layer, carry):
        forward_corners(layer)
        assemble(layer)
        for k in range(count):
            cut_layer(k, layer)
        fields = [leave(k, layer) for k in range(count)]
        for k, (re, im) in enumerate(hop(fields, phases[0], phases[1], pairs)):
            waves[k, layer + 1, 0] = re
            waves[k, layer + 1, 1] = im
        return carry

    lax.fori_loop(0, last, onward, 0)

    def record(k, layer, back_re, back_im):
        wave_re, wave_im = waves[k, layer, 0], waves[k, layer, 1]
        shift = row_place(offsets[0, 0, k, 0], whole, width)[1]
        turn = lane_place(offsets[0, 0, k, 1])[1]
        terms = (wave_re * back_re + wave_im * back_im, wave_re * back_im - wave_im * back_re)
        for c in range(2):
            blocks = jnp.stack([terms[c][:, j * LANES : j * LANES + LANES] for j in range(wide)])
            blocks = spread(blocks, turn, 2, LANES)
            for j in range(rounds):
                part = spread(blocks[j].reshape(width // 8, 8, LANES), shift, 1, 8)
                spans[k, c, j, pl.ds(pad // 8, width // 8 + 1)] = part

    def summed(c, block, start, size):
        found = None
        for k in range(count):
            base = row_place(offsets[0, 0, k, 0], whole, width)[0]
            first = lane_place(offsets[0, 0, k, 1])[0]
            at = (pad + start) // 8 - base
            term = spans[k, c, lax.rem(block + rounds - first, rounds), pl.ds(at, size // 8)]
            found = term if found is None else found + term
        return found.reshape(size, LANES)

    def settle(layer):
        for start, size, d in pieces:
            blocks = [[summed(c, j, start, size) for j in range(wide)] for c in range(2)]
            outer_re, outer_im = (summed(c, wide, start, size) for c in range(2))
            to_right, to_left = choose(outer_re, swapped(outer_im)), choose(swapped(outer_re), outer_im)
            if d is None:
                for c in range(2):
                    for j in range(wide):
                        total[c, layer, :, j * LANES : j * LANES + LANES] = blocks[c][j]
                gcol_out[layer, 0] = to_right
                gcol_out[layer, 1] = to_left
            else:
                for half, packs in enumerate((ends_of(blocks), middle_of(blocks))):
                    for i in range(2):
                        grow_out[layer, half, i, 1 - d] = packs[i]
                gcorner_out[layer, 0, 1 - d] = to_right
                gcorner_out[layer, 1, 1 - d] = to_left
        for side in range(2):
            gcorner_copy(layer, side).start()
        for d in range(2):
            grow_copy(layer, 1, d).start()
        for side in range(2):
            gcol_copy(layer, side).start()

    def pass_on(layer):
        for side in range(2):
            gcorner_copy(layer, side).wait_recv()
        for d in range(2):
            for side in range(2):
                grow_out[layer, 0, side, d] += gcorner_in[layer, side, d]
            grow_copy(layer, 0, d).start()

    forward_corners(last)
    assemble(last)
    for k in range(count):
        cut_layer(k, last)
    for k in range(count):
        far_re, far_im = forward(*leave(k, last), pairs)
        misfit = far_re * far_re + far_im * far_im - ordered[k]
        back_re, back_im = inverse(misfit * far_re, misfit * far_im, pairs)
        record(k, last, back_re, back_im)
        waves[k, last, 0] = back_re
        waves[k, last, 1] = back_im
    settle(last)

    def backward(step, carry):
        layer = last - step
        fields = []
        for k in range(count):
            back_re, back_im = waves[k, layer, 0], waves[k, layer, 1]
            slab_re, slab_im = windows[k, layer, 0], windows[k, layer, 1]
            fields.append(complex_product(back_re, back_im, slab_re, -slab_im))
        backs = hop(fields, phases[0], -phases[1], pairs)
        pass_on(layer)
        for k, (re, im) in enumerate(backs):
            record(k, layer - 1, re, im)
            waves[k, layer - 1, 0] = re
            waves[k, layer - 1, 1] = im
        settle(layer - 1)
        return carry

    lax.fori_loop(0, last, backward, 0)
    pass_on(0)

    def stores(layer):
        return (
            pltpu.make_async_copy(total.at[:, layer], gradient.at[:, layer], store_sem.at[0, layer]),
            pltpu.make_async_copy(cells.at[:, layer], updated.at[:, layer], store_sem.at[1, layer]),
        )

    def finish(step, carry):
        layer = last - step
        for side in range(2):
            gcol_copy(layer, side).wait_recv()
        for half in (1, 0):
            for d in range(2):
                grow_copy(layer, half, d).wait_recv()
        spots = ((0, HALO, 0), (HALO, tall - 2 * HALO, None), (tall - HALO, HALO, 1))
        for start, size, d in spots:
            rows = pl.ds(start, size)
            sums = lane_blocks(total, layer, rows)
            if d is not None:
                added = unpacked(*(grow_in[layer, half, i, d] for half in range(2) for i in range(2)))
                sums = [[sums[c][j] + added[c][j] for j in range(wide)] for c in range(2)]
            l, r = gcol_in[layer, 0, rows, :], gcol_in[layer, 1, rows, :]
            zero = jnp.zeros_like(l)
            sums[0][0] += choose(l, zero)
            sums[1][0] += choose(swapped(l), zero)
            sums[0][wide - 1] += choose(zero, swapped(r))
            sums[1][wide - 1] += choose(zero, r)
            for c in range(2):
                for j in range(wide):
                    lanes = pl.ds(j * LANES, LANES)
                    total[c, layer, rows, lanes] = sums[c][j]
                    cells[c, layer, rows, lanes] -= descent_rate * sums[c][j]
        for store in stores(layer):
            store.start()
        return carry

    lax.fori_loop(0, layers, finish, 0)

    def close(layer, carry):
        for d in range(2):
            for half in range(2):
                row_copy(layer, half, d).wait_send()
                grow_copy(layer, half, d).wait_send()
            col_copy(layer, d).wait_send()
            corner_copy(layer, d).wait_send()
            gcol_copy(layer, d).wait_send()
            gcorner_copy(layer, d).wait_send()
        for store in stores(layer):
            store.wait()
        return carry

    lax.fori_loop(0, layers, close, 0)


def on_device(object_slices, positions, intensities, probe, propagator):
    count, width = intensities.shape[2], intensities.shape[-1]
    layers, tall, broad = object_slices.shape[1:]
    rounds = broad // LANES + 1
    tables = jnp.asarray(half_tables(width))
    anywhere = pl.BlockSpec(memory_space=pl.ANY)
    like = jax.ShapeDtypeStruct(object_slices.shape, object_slices.dtype)
    f32 = functools.partial(pltpu.VMEM, dtype=jnp.float32)
    strip, side, corner = (layers, 2, 2, 2, HALO, LANES), (layers, 2, tall, LANES), (layers, 2, 2, HALO, LANES)
    dma = pltpu.SemaphoreType.DMA
    return tuple(
        pl.pallas_call(
            step_kernel,
            out_shape=[like, like],
            in_specs=[pl.BlockSpec(memory_space=pltpu.SMEM)] + [anywhere] * 5,
            out_specs=[anywhere] * 2,
            scratch_shapes=[
                pltpu.VMEM(tables.shape, tables.dtype),
                f32(object_slices.shape),
                f32((count, width, width)),
                f32((count, width, width)),
                f32((width, width)),
                f32((2, width, width)),
                f32((count, layers, 2, width, width)),
                f32((count, layers, 2, width, width)),
                f32((2, rounds, (tall + 2 * HALO) // 8, 8, LANES)),
                f32((count, 2, rounds, (width + 4 * HALO) // 8 + 1, 8, LANES)),
                f32(object_slices.shape),
                f32(strip), f32(strip), f32(side), f32(side), f32(corner),
                f32(strip), f32(strip), f32(side), f32(side), f32(corner), f32(corner),
                dma((3 + count,)), dma((layers,)), dma((2, layers)),
                dma((2, layers, 2, 2)), dma((2, layers, 2)), dma((2, layers, 2)),
                dma((2, layers, 2, 2)), dma((2, layers, 2)), dma((2, layers, 2)),
            ],
            compiler_params=pltpu.CompilerParams(
                collective_id=0, has_side_effects=True, vmem_limit_bytes=58 * 2**20
            ),
        )(positions, object_slices, intensities.reshape(count, width, width), probe, propagator, tables)
    )


def solution(mesh):
    return jax.shard_map(
        on_device,
        mesh=mesh,
        in_specs=(
            P(None, None, "row", "col"),
            P("row", "col", None, None),
            P("row", "col", None, None, None),
            P(),
            P(),
        ),
        out_specs=(P(None, None, "row", "col"), P(None, None, "row", "col")),
        check_vma=False,
    )
```

time: 111 us -> 77.4 us (0.70)
  waiting for transfers between devices: 48.9 us -> 0 us
  Pallas kernels: 37.7 us -> 72.2 us
  starting transfers between devices: 16.2 us -> 0 us
  other arithmetic: 2.98 us -> 0 us
    ppermute x12 -> x0, waiting for transfers between devices: 48.9 us -> none  [passed_along(): return lax.ppermute(block, axis, route)]
    pallas_call x4 -> x1, Pallas kernels: 37.7 us -> 72.2 us  [on_device(): pl.pallas_call(step_kernel, out_shape=[like, like], in_specs=[pl.BlockSpe...]
    ppermute x12 -> x0, starting transfers between devices: 16.2 us -> none  [passed_along(): return lax.ppermute(block, axis, route)]
    unnamed x25 -> x4, local copies, waits for them, and re-layouts: 1.58 us -> 4.52 us
    concatenate x4 -> x0, other arithmetic: 2.15 us -> none  [the longest x2 1.11 us: packed(): head = jnp.concatenate([cells[0, ..., :HALO], cells[1, ..., :HALO]], -1)]
    slice x1 -> x0, local copies, waits for them, and re-layouts: 1.42 us -> none  [on_device(): below = passed_along(object_slices[:, :, :HALO], 'row', -1)]
  transfers between devices with their start and end apart: 12 -> 0, of which waited for: 8 -> 0; matrix products, arithmetic and copies ran while one was open for 4% -> 0% of each run, Pallas kernels for 6% -> 0%
where the time goes in v1:
time: 77.4 us
  Pallas kernels  72.2 us (93%)
  local copies, waits for them, and re-layouts  4.52 us (6%)
    pallas_call x1, Pallas kernels, on_device(): pl.pallas_call(step_kernel, out_shape=[like, like], in_specs=[pl.BlockSpe...  72.2 us
    unnamed x4, local copies, waits for them, and re-layouts  4.52 us

profile of v1, /device:TPU:0, one launch (start us, length us, event | category | flops | bytes accessed | tf_op | source)
XLA Modules:
  0.0 77.4 jit_solution(4854614211104844181)
XLA Ops:
  0.6 72.2 %shard_map.77 = (f32[2,4,256,256]{3,2,1,0:T(8,128)}, f32[2,4,256,256]{3,2,1,0:T(8,128)}) custom-call(s32[1,1,2,2]{3,2,1,0:T(2,128)} %offsets.1, f32[2,4,256,256]{3,2,1,0:T(8,128)} %objects.1, f32[2,256,256]{2,1,0:T(8,128)} %bitcast.1, f32[2,256,256]{2,1,0:T(8,128)} %probe.1, f32[256,256]{1,0:T(8,128)} %propagator.1, ...), custom_call_target="tpu_custom_call" | custom-call | tf_op jit(solution)/shard_map/pallas_call | solution.py:495
  72.8 0.0 copy-start
  72.8 3.2 %copy.10 = f32[2,4,256,256]{3,2,1,0:T(8,128)} copy(f32[2,4,256,256]{3,2,1,0:T(8,128)} %get-tuple-element.4) | data formatting | bytes 4194304
  76.0 0.0 copy-done
  76.0 1.3 %copy.11 = f32[2,4,256,256]{3,2,1,0:T(8,128)} copy(f32[2,4,256,256]{3,2,1,0:T(8,128)S(1)} %copy-done) | data formatting | bytes 4194304
Async XLA Ops:
  72.8 3.2 %copy-start = (f32[2,4,256,256]{3,2,1,0:T(8,128)S(1)}, f32[2,4,256,256]{3,2,1,0:T(8,128)}, u32[]{:S(2)}) copy-start(f32[2,4,256,256]{3,2,1,0:T(8,128)} %get-tuple-element.5) | copy-start | bytes 6291460

commit v2 on v1

--- a/solution.py
+++ b/solution.py
@@ -171,12 +171,12 @@
 
 
 def step_kernel(
-    offsets, objects, intensities, probe, propagator, tables_in,
+    offsets_in, objects, intensities, probe, propagator, tables_in,
     gradient, updated,
-    tables, cells, measured, ordered, phase, phases, waves, windows, slab, spans, total,
+    offsets, tables, cells, measured, ordered, phase, phases, waves, windows, slab, spans,
     row_out, row_in, col_out, col_in, corner_in,
     grow_out, grow_in, gcol_out, gcol_in, gcorner_out, gcorner_in,
-    load_sem, slice_sem, store_sem, row_sem, col_sem, corner_sem, grow_sem, gcol_sem, gcorner_sem,
+    load_sem, slice_sem, row_sem, col_sem, corner_sem, grow_sem, gcol_sem, gcorner_sem,
 ):
     count, width = measured.shape[0], measured.shape[-1]
     layers, tall = cells.shape[1:3]
@@ -191,6 +191,7 @@
     below, above = lax.rem(row + 1, rows_n), lax.rem(row + rows_n - 1, rows_n)
     right, left = lax.rem(col + 1, cols_n), lax.rem(col + cols_n - 1, cols_n)
     row_to = ((below, col), (above, col))
+    soon = lax.rem(lax.div(row + 1, 2), 2)
     col_to = ((row, right), (row, left))
 
     def send(src, dst, sems, where, target):
@@ -201,7 +202,8 @@
 
     def row_copy(layer, half, d):
         where = (layer, half, slice(None), d)
-        return send(row_out.at[where], row_in.at[where], row_sem, (layer, half, d), row_to[d])
+        target = (lax.rem(row + rows_n + 1 - 2 * d, rows_n), col)
+        return send(row_out.at[where], row_in.at[where], row_sem, (layer, half, d), target)
 
     def col_copy(layer, side):
         return send(col_out.at[layer, side], col_in.at[layer, side], col_sem, (layer, side), col_to[side])
@@ -226,7 +228,8 @@
         pltpu.make_async_copy(propagator, phase, load_sem.at[0]),
         pltpu.make_async_copy(tables_in, tables, load_sem.at[1]),
         pltpu.make_async_copy(intensities, measured, load_sem.at[2]),
-    ] + [pltpu.make_async_copy(probe, waves.at[k, 0], load_sem.at[3 + k]) for k in range(count)]
+        pltpu.make_async_copy(offsets_in, offsets, load_sem.at[3]),
+    ] + [pltpu.make_async_copy(probe, waves.at[k, 0], load_sem.at[4 + k]) for k in range(count)]
 
     def slice_load(layer):
         return pltpu.make_async_copy(objects.at[:, layer], cells.at[:, layer], slice_sem.at[layer])
@@ -236,13 +239,11 @@
         pl.semaphore_signal(barrier, inc=1, device_id=target, device_id_type=pl.DeviceIdType.MESH)
     for layer in range(layers):
         slice_load(layer).start()
-    for load in loads:
-        load.start()
 
     def lane_blocks(ref, layer, rows):
         return [[ref[c, layer, rows, pl.ds(j * LANES, LANES)] for j in range(wide)] for c in range(2)]
 
-    def pack(layer, carry):
+    def pack(layer):
         slice_load(layer).wait()
         for d, at in enumerate((tall - HALO, 0)):
             strip = lane_blocks(cells, layer, pl.ds(at, HALO))
@@ -252,20 +253,30 @@
         head, tail = ends_of(lane_blocks(cells, layer, pl.ds(0, tall)))
         col_out[layer, 0] = tail
         col_out[layer, 1] = head
+
+    def launch(layer):
+        for half in range(2):
+            row_copy(layer, half, soon).start()
+        for side in range(2):
+            col_copy(layer, side).start()
+
+    def pack_and_launch(layer, carry):
+        pack(layer)
+        launch(layer)
         return carry
 
-    lax.fori_loop(0, layers, pack, 0)
+    def launch_late(layer, carry):
+        for half in range(2):
+            row_copy(layer, half, 1 - soon).start()
+        return carry
+
+    pack(0)
     pl.semaphore_wait(barrier, 4)
-
-    def launch(layer, carry):
-        for half in range(2):
-            for d in range(2):
-                row_copy(layer, half, d).start()
-        for side in range(2):
-            col_copy(layer, side).start()
-        return carry
-
-    lax.fori_loop(0, layers, launch, 0)
+    launch(0)
+    for load in loads:
+        load.start()
+    lax.fori_loop(1, layers, pack_and_launch, 0)
+    lax.fori_loop(0, layers, launch_late, 0)
 
     def pairs(index):
         return tables[0, index], tables[1, index]
@@ -330,16 +341,17 @@
         )
 
     def onward(layer, carry):
-        forward_corners(layer)
         assemble(layer)
         for k in range(count):
             cut_layer(k, layer)
+        forward_corners(layer + 1)
         fields = [leave(k, layer) for k in range(count)]
         for k, (re, im) in enumerate(hop(fields, phases[0], phases[1], pairs)):
             waves[k, layer + 1, 0] = re
             waves[k, layer + 1, 1] = im
         return carry
 
+    forward_corners(0)
     lax.fori_loop(0, last, onward, 0)
 
     def record(k, layer, back_re, back_im):
@@ -372,7 +384,7 @@
             if d is None:
                 for c in range(2):
                     for j in range(wide):
-                        total[c, layer, :, j * LANES : j * LANES + LANES] = blocks[c][j]
+                        gradient[c, layer, :, j * LANES : j * LANES + LANES] = blocks[c][j]
                 gcol_out[layer, 0] = to_right
                 gcol_out[layer, 1] = to_left
             else:
@@ -396,7 +408,6 @@
                 grow_out[layer, 0, side, d] += gcorner_in[layer, side, d]
             grow_copy(layer, 0, d).start()
 
-    forward_corners(last)
     assemble(last)
     for k in range(count):
         cut_layer(k, last)
@@ -428,12 +439,6 @@
     lax.fori_loop(0, last, backward, 0)
     pass_on(0)
 
-    def stores(layer):
-        return (
-            pltpu.make_async_copy(total.at[:, layer], gradient.at[:, layer], store_sem.at[0, layer]),
-            pltpu.make_async_copy(cells.at[:, layer], updated.at[:, layer], store_sem.at[1, layer]),
-        )
-
     def finish(step, carry):
         layer = last - step
         for side in range(2):
@@ -444,7 +449,7 @@
         spots = ((0, HALO, 0), (HALO, tall - 2 * HALO, None), (tall - HALO, HALO, 1))
         for start, size, d in spots:
             rows = pl.ds(start, size)
-            sums = lane_blocks(total, layer, rows)
+            sums = lane_blocks(gradient, layer, rows)
             if d is not None:
                 added = unpacked(*(grow_in[layer, half, i, d] for half in range(2) for i in range(2)))
                 sums = [[sums[c][j] + added[c][j] for j in range(wide)] for c in range(2)]
@@ -457,10 +462,8 @@
             for c in range(2):
                 for j in range(wide):
                     lanes = pl.ds(j * LANES, LANES)
-                    total[c, layer, rows, lanes] = sums[c][j]
-                    cells[c, layer, rows, lanes] -= descent_rate * sums[c][j]
-        for store in stores(layer):
-            store.start()
+                    gradient[c, layer, rows, lanes] = sums[c][j]
+                    updated[c, layer, rows, lanes] = cells[c, layer, rows, lanes] - descent_rate * sums[c][j]
         return carry
 
     lax.fori_loop(0, layers, finish, 0)
@@ -474,11 +477,20 @@
             corner_copy(layer, d).wait_send()
             gcol_copy(layer, d).wait_send()
             gcorner_copy(layer, d).wait_send()
-        for store in stores(layer):
-            store.wait()
         return carry
 
     lax.fori_loop(0, layers, close, 0)
+
+
+def publish_kernel(gradient, updated, gradient_out, updated_out, sems):
+    copies = (
+        pltpu.make_async_copy(gradient, gradient_out, sems.at[0]),
+        pltpu.make_async_copy(updated, updated_out, sems.at[1]),
+    )
+    for copy in copies:
+        copy.start()
+    for copy in copies:
+        copy.wait()
 
 
 def on_device(object_slices, positions, intensities, probe, propagator):
@@ -487,38 +499,46 @@
     rounds = broad // LANES + 1
     tables = jnp.asarray(half_tables(width))
     anywhere = pl.BlockSpec(memory_space=pl.ANY)
-    like = jax.ShapeDtypeStruct(object_slices.shape, object_slices.dtype)
     f32 = functools.partial(pltpu.VMEM, dtype=jnp.float32)
     strip, side, corner = (layers, 2, 2, 2, HALO, LANES), (layers, 2, tall, LANES), (layers, 2, 2, HALO, LANES)
     dma = pltpu.SemaphoreType.DMA
+    held = pltpu.VMEM(object_slices.shape, object_slices.dtype)
+    pair = [held, held]
+    found = pl.pallas_call(
+        step_kernel,
+        out_shape=pair,
+        in_specs=[anywhere] * 6,
+        out_specs=[pl.BlockSpec(memory_space=pltpu.VMEM)] * 2,
+        scratch_shapes=[
+            pltpu.SMEM(positions.shape, positions.dtype),
+            pltpu.VMEM(tables.shape, tables.dtype),
+            f32(object_slices.shape),
+            f32((count, width, width)),
+            f32((count, width, width)),
+            f32((width, width)),
+            f32((2, width, width)),
+            f32((count, layers, 2, width, width)),
+            f32((count, layers, 2, width, width)),
+            f32((2, rounds, (tall + 2 * HALO) // 8, 8, LANES)),
+            f32((count, 2, rounds, (width + 4 * HALO) // 8 + 1, 8, LANES)),
+            f32(strip), f32(strip), f32(side), f32(side), f32(corner),
+            f32(strip), f32(strip), f32(side), f32(side), f32(corner), f32(corner),
+            dma((4 + count,)), dma((layers,)),
+            dma((2, layers, 2, 2)), dma((2, layers, 2)), dma((2, layers, 2)),
+            dma((2, layers, 2, 2)), dma((2, layers, 2)), dma((2, layers, 2)),
+        ],
+        compiler_params=pltpu.CompilerParams(collective_id=0, has_side_effects=True, vmem_limit_bytes=54 * 2**20),
+    )(positions, object_slices, intensities.reshape(count, width, width), probe, propagator, tables)
+    like = jax.ShapeDtypeStruct(object_slices.shape, object_slices.dtype)
     return tuple(
         pl.pallas_call(
-            step_kernel,
+            publish_kernel,
             out_shape=[like, like],
-            in_specs=[pl.BlockSpec(memory_space=pltpu.SMEM)] + [anywhere] * 5,
+            in_specs=[pl.BlockSpec(memory_space=pltpu.VMEM)] * 2,
             out_specs=[anywhere] * 2,
-            scratch_shapes=[
-                pltpu.VMEM(tables.shape, tables.dtype),
-                f32(object_slices.shape),
-                f32((count, width, width)),
-                f32((count, width, width)),
-                f32((width, width)),
-                f32((2, width, width)),
-                f32((count, layers, 2, width, width)),
-                f32((count, layers, 2, width, width)),
-                f32((2, rounds, (tall + 2 * HALO) // 8, 8, LANES)),
-                f32((count, 2, rounds, (width + 4 * HALO) // 8 + 1, 8, LANES)),
-                f32(object_slices.shape),
-                f32(strip), f32(strip), f32(side), f32(side), f32(corner),
-                f32(strip), f32(strip), f32(side), f32(side), f32(corner), f32(corner),
-                dma((3 + count,)), dma((layers,)), dma((2, layers)),
-                dma((2, layers, 2, 2)), dma((2, layers, 2)), dma((2, layers, 2)),
-                dma((2, layers, 2, 2)), dma((2, layers, 2)), dma((2, layers, 2)),
-            ],
-            compiler_params=pltpu.CompilerParams(
-                collective_id=0, has_side_effects=True, vmem_limit_bytes=58 * 2**20
-            ),
-        )(positions, object_slices, intensities.reshape(count, width, width), probe, propagator, tables)
+            scratch_shapes=[dma((2,))],
+            compiler_params=pltpu.CompilerParams(vmem_limit_bytes=2**20),
+        )(*(pltpu.with_memory_space_constraint(v, pltpu.VMEM) for v in found))
     )
 
 

time: 77.4 us -> 66.4 us (0.86)
  Pallas kernels: 72.2 us -> 65.6 us
  local copies, waits for them, and re-layouts: 4.52 us -> 0 us
    pallas_call x1 -> x2, Pallas kernels: 72.2 us -> 65.6 us  [the longest x1 63.6 us: on_device(): pl.pallas_call(step_kernel, out_shape=pair, in_specs=[anywhere] * 6, out_...]
    unnamed x4 -> x0, local copies, waits for them, and re-layouts: 4.52 us -> none
where the time goes in v2:
time: 66.4 us; the launch traced here: 66.2 us
  Pallas kernels  65.6 us (99%)
    pallas_call x1, Pallas kernels, on_device(): pl.pallas_call(step_kernel, out_shape=pair, in_specs=[anywhere] * 6, out_...  63.6 us
    pallas_call x1, Pallas kernels, on_device(): pl.pallas_call(publish_kernel, out_shape=[like, like], in_specs=[pl.Block...  2.03 us

profile of v2, /device:TPU:0, one launch (start us, length us, event | category | flops | bytes accessed | tf_op | source)
XLA Modules:
  0.0 66.2 jit_solution(2093081516483884598)
XLA Ops:
  0.6 63.6 %shard_map.77 = (f32[2,4,256,256]{3,2,1,0:T(8,128)S(1)}, f32[2,4,256,256]{3,2,1,0:T(8,128)S(1)}) custom-call(s32[1,1,2,2]{3,2,1,0:T(2,128)} %offsets_in.1, f32[2,4,256,256]{3,2,1,0:T(8,128)} %objects.1, f32[2,256,256]{2,1,0:T(8,128)} %bitcast.1, f32[2,256,256]{2,1,0:T(8,128)} %probe.1, f32[256,256]{1,0:T(8,128)} %propagator.1, ...), custom_call_target="tpu_custom_call" | custom-call | tf_op jit(solution)/shard_map/pallas_call | solution.py:507
  64.2 2.0 %shard_map.78 = (f32[2,4,256,256]{3,2,1,0:T(8,128)}, f32[2,4,256,256]{3,2,1,0:T(8,128)}) custom-call(f32[2,4,256,256]{3,2,1,0:T(8,128)S(1)} %get-tuple-element.4.gradient, f32[2,4,256,256]{3,2,1,0:T(8,128)S(1)} %get-tuple-element.5.updated), custom_call_target="tpu_custom_call" | custom-call | tf_op jit(solution)/shard_map/pallas_call | solution.py:534

commit v3 on v2

--- a/solution.py
+++ b/solution.py
@@ -191,7 +191,6 @@
     below, above = lax.rem(row + 1, rows_n), lax.rem(row + rows_n - 1, rows_n)
     right, left = lax.rem(col + 1, cols_n), lax.rem(col + cols_n - 1, cols_n)
     row_to = ((below, col), (above, col))
-    soon = lax.rem(lax.div(row + 1, 2), 2)
     col_to = ((row, right), (row, left))
 
     def send(src, dst, sems, where, target):
@@ -214,7 +213,8 @@
 
     def grow_copy(layer, half, d):
         where = (layer, half, slice(None), d)
-        return send(grow_out.at[where], grow_in.at[where], grow_sem, (layer, half, d), row_to[d])
+        target = (lax.rem(row + rows_n + 1 - 2 * d, rows_n), col)
+        return send(grow_out.at[where], grow_in.at[where], grow_sem, (layer, half, d), target)
 
     def gcol_copy(layer, side):
         return send(gcol_out.at[layer, side], gcol_in.at[layer, side], gcol_sem, (layer, side), col_to[side])
@@ -256,27 +256,26 @@
 
     def launch(layer):
         for half in range(2):
-            row_copy(layer, half, soon).start()
-        for side in range(2):
-            col_copy(layer, side).start()
+            for d in range(2):
+                row_copy(layer, half, d).start()
 
     def pack_and_launch(layer, carry):
         pack(layer)
         launch(layer)
+        launch_sides(layer)
         return carry
 
-    def launch_late(layer, carry):
-        for half in range(2):
-            row_copy(layer, half, 1 - soon).start()
-        return carry
+    def launch_sides(layer):
+        for side in range(2):
+            col_copy(layer, side).start()
 
     pack(0)
     pl.semaphore_wait(barrier, 4)
     launch(0)
+    launch_sides(0)
     for load in loads:
         load.start()
     lax.fori_loop(1, layers, pack_and_launch, 0)
-    lax.fori_loop(0, layers, launch_late, 0)
 
     def pairs(index):
         return tables[0, index], tables[1, index]
@@ -295,33 +294,33 @@
                 spans[k, c, j, pl.ds(0, pad // 8)] = blank
                 spans[k, c, j, pl.ds((pad + width) // 8 + 1, pad // 8)] = blank
 
-    pieces = ((0, HALO, 0), (HALO, tall, None), (HALO + tall, HALO, 1))
-
-    def forward_corners(layer):
+    def forward_corners(layer, more):
         for d in range(2):
             row_copy(layer, 0, d).wait_recv()
         for side in range(2):
             corner_copy(layer, side).start()
+        if more:
+            launch_sides(layer + 1)
 
     def assemble(layer):
-        for d in range(2):
-            row_copy(layer, 1, d).wait_recv()
-        for side in range(2):
-            col_copy(layer, side).wait_recv()
-            corner_copy(layer, side).wait_recv()
-        for start, size, d in pieces:
+        def place(start, size, blocks, l, r):
             rows, tiles = pl.ds(start // 8, size // 8), (size // 8, 8, LANES)
-            if d is None:
-                blocks = lane_blocks(cells, layer, pl.ds(0, tall))
-                l, r = col_in[layer, 0], col_in[layer, 1]
-            else:
-                blocks = unpacked(*(row_in[layer, half, i, d] for half in range(2) for i in range(2)))
-                l, r = corner_in[layer, 0, d], corner_in[layer, 1, d]
             for c in range(2):
                 for j in range(wide):
                     slab[c, j, rows] = blocks[c][j].reshape(tiles)
             slab[0, wide, rows] = choose(r, swapped(l)).reshape(tiles)
             slab[1, wide, rows] = choose(swapped(r), l).reshape(tiles)
+
+        for side in range(2):
+            col_copy(layer, side).wait_recv()
+        place(HALO, tall, lane_blocks(cells, layer, pl.ds(0, tall)), col_in[layer, 0], col_in[layer, 1])
+        for d in range(2):
+            row_copy(layer, 1, d).wait_recv()
+        for side in range(2):
+            corner_copy(layer, side).wait_recv()
+        for d, start in enumerate((0, HALO + tall)):
+            blocks = unpacked(*(row_in[layer, half, i, d] for half in range(2) for i in range(2)))
+            place(start, HALO, blocks, corner_in[layer, 0, d], corner_in[layer, 1, d])
 
     def cut_layer(k, layer):
         base, shift = row_place(offsets[0, 0, k, 0], whole, width)
@@ -344,14 +343,14 @@
         assemble(layer)
         for k in range(count):
             cut_layer(k, layer)
-        forward_corners(layer + 1)
-        fields = [leave(k, layer) for k in range(count)]
-        for k, (re, im) in enumerate(hop(fields, phases[0], phases[1], pairs)):
+            if k == 0:
+                forward_corners(layer + 1, False)
+            ((re, im),) = hop([leave(k, layer)], phases[0], phases[1], pairs)
             waves[k, layer + 1, 0] = re
             waves[k, layer + 1, 1] = im
         return carry
 
-    forward_corners(0)
+    forward_corners(0, False)
     lax.fori_loop(0, last, onward, 0)
 
     def record(k, layer, back_re, back_im):
@@ -377,27 +376,29 @@
         return found.reshape(size, LANES)
 
     def settle(layer):
-        for start, size, d in pieces:
+        def sums(start, size):
             blocks = [[summed(c, j, start, size) for j in range(wide)] for c in range(2)]
             outer_re, outer_im = (summed(c, wide, start, size) for c in range(2))
-            to_right, to_left = choose(outer_re, swapped(outer_im)), choose(swapped(outer_re), outer_im)
-            if d is None:
-                for c in range(2):
-                    for j in range(wide):
-                        gradient[c, layer, :, j * LANES : j * LANES + LANES] = blocks[c][j]
-                gcol_out[layer, 0] = to_right
-                gcol_out[layer, 1] = to_left
-            else:
-                for half, packs in enumerate((ends_of(blocks), middle_of(blocks))):
-                    for i in range(2):
-                        grow_out[layer, half, i, 1 - d] = packs[i]
-                gcorner_out[layer, 0, 1 - d] = to_right
-                gcorner_out[layer, 1, 1 - d] = to_left
+            return blocks, (choose(outer_re, swapped(outer_im)), choose(swapped(outer_re), outer_im))
+
+        for d, start in enumerate((0, HALO + tall)):
+            blocks, outer = sums(start, HALO)
+            for half, packs in enumerate((ends_of(blocks), middle_of(blocks))):
+                for i in range(2):
+                    grow_out[layer, half, i, 1 - d] = packs[i]
+            for side in range(2):
+                gcorner_out[layer, side, 1 - d] = outer[side]
         for side in range(2):
             gcorner_copy(layer, side).start()
         for d in range(2):
             grow_copy(layer, 1, d).start()
-        for side in range(2):
+
+        blocks, outer = sums(HALO, tall)
+        for c in range(2):
+            for j in range(wide):
+                gradient[c, layer, :, j * LANES : j * LANES + LANES] = blocks[c][j]
+        for side in range(2):
+            gcol_out[layer, side] = outer[side]
             gcol_copy(layer, side).start()
 
     def pass_on(layer):
@@ -406,15 +407,18 @@
         for d in range(2):
             for side in range(2):
                 grow_out[layer, 0, side, d] += gcorner_in[layer, side, d]
+        for d in range(2):
             grow_copy(layer, 0, d).start()
 
     assemble(last)
     for k in range(count):
         cut_layer(k, last)
+    leaving = [leave(k, last) for k in range(count)]
+    far_re, far_im = forward(*(jnp.concatenate([v[c] for v in leaving], 1) for c in range(2)), pairs)
+    misfit = far_re * far_re + far_im * far_im - ordered[...].reshape(far_re.shape)
+    backs = inverse(misfit * far_re, misfit * far_im, pairs)
     for k in range(count):
-        far_re, far_im = forward(*leave(k, last), pairs)
-        misfit = far_re * far_re + far_im * far_im - ordered[k]
-        back_re, back_im = inverse(misfit * far_re, misfit * far_im, pairs)
+        back_re, back_im = (v[:, k * width : (k + 1) * width] for v in backs)
         record(k, last, back_re, back_im)
         waves[k, last, 0] = back_re
         waves[k, last, 1] = back_im
@@ -438,7 +442,6 @@
 
     lax.fori_loop(0, last, backward, 0)
     pass_on(0)
-
     def finish(step, carry):
         layer = last - step
         for side in range(2):
@@ -483,10 +486,11 @@
 
 
 def publish_kernel(gradient, updated, gradient_out, updated_out, sems):
-    copies = (
-        pltpu.make_async_copy(gradient, gradient_out, sems.at[0]),
-        pltpu.make_async_copy(updated, updated_out, sems.at[1]),
-    )
+    copies = [
+        pltpu.make_async_copy(held.at[:, layer], out.at[:, layer], sems.at[i, layer])
+        for i, (held, out) in enumerate(((gradient, gradient_out), (updated, updated_out)))
+        for layer in range(gradient.shape[1])
+    ]
     for copy in copies:
         copy.start()
     for copy in copies:
@@ -536,7 +540,7 @@
             out_shape=[like, like],
             in_specs=[pl.BlockSpec(memory_space=pltpu.VMEM)] * 2,
             out_specs=[anywhere] * 2,
-            scratch_shapes=[dma((2,))],
+            scratch_shapes=[dma((2, layers))],
             compiler_params=pltpu.CompilerParams(vmem_limit_bytes=2**20),
         )(*(pltpu.with_memory_space_constraint(v, pltpu.VMEM) for v in found))
     )

time: 66.4 us -> 65.1 us (0.980)
  Pallas kernels: 65.6 us -> 64.3 us
    pallas_call x1, Pallas kernels: 63.6 us -> 62.2 us  [on_device(): pl.pallas_call(step_kernel, out_shape=pair, in_specs=[anywhere] * 6, out_...]
where the time goes in v3:
time: 65.1 us; the launch traced here: 64.9 us
  Pallas kernels  64.3 us (99%)
    pallas_call x1, Pallas kernels, on_device(): pl.pallas_call(step_kernel, out_shape=pair, in_specs=[anywhere] * 6, out_...  62.2 us
    pallas_call x1, Pallas kernels, on_device(): pl.pallas_call(publish_kernel, out_shape=[like, like], in_specs=[pl.Block...  2.07 us

profile of v3, /device:TPU:0, one launch (start us, length us, event | category | flops | bytes accessed | tf_op | source)
XLA Modules:
  0.0 64.9 jit_solution(12694928851268064333)
XLA Ops:
  0.6 62.2 %shard_map.77 = (f32[2,4,256,256]{3,2,1,0:T(8,128)S(1)}, f32[2,4,256,256]{3,2,1,0:T(8,128)S(1)}) custom-call(s32[1,1,2,2]{3,2,1,0:T(2,128)} %offsets_in.1, f32[2,4,256,256]{3,2,1,0:T(8,128)} %objects.1, f32[2,256,256]{2,1,0:T(8,128)} %bitcast.1, f32[2,256,256]{2,1,0:T(8,128)} %probe.1, f32[256,256]{1,0:T(8,128)} %propagator.1, ...), custom_call_target="tpu_custom_call" | custom-call | tf_op jit(solution)/shard_map/pallas_call | solution.py:511
  62.9 2.1 %shard_map.78 = (f32[2,4,256,256]{3,2,1,0:T(8,128)}, f32[2,4,256,256]{3,2,1,0:T(8,128)}) custom-call(f32[2,4,256,256]{3,2,1,0:T(8,128)S(1)} %get-tuple-element.4.gradient, f32[2,4,256,256]{3,2,1,0:T(8,128)S(1)} %get-tuple-element.5.updated), custom_call_target="tpu_custom_call" | custom-call | tf_op jit(solution)/shard_map/pallas_call | solution.py:538

commit v4 on v3

--- a/solution.py
+++ b/solution.py
@@ -255,8 +255,8 @@
         col_out[layer, 1] = head
 
     def launch(layer):
-        for half in range(2):
-            for d in range(2):
+        for d in range(2):
+            for half in range(2):
                 row_copy(layer, half, d).start()
 
     def pack_and_launch(layer, carry):
@@ -294,13 +294,11 @@
                 spans[k, c, j, pl.ds(0, pad // 8)] = blank
                 spans[k, c, j, pl.ds((pad + width) // 8 + 1, pad // 8)] = blank
 
-    def forward_corners(layer, more):
+    def forward_corners(layer):
         for d in range(2):
             row_copy(layer, 0, d).wait_recv()
         for side in range(2):
             corner_copy(layer, side).start()
-        if more:
-            launch_sides(layer + 1)
 
     def assemble(layer):
         def place(start, size, blocks, l, r):
@@ -344,17 +342,20 @@
         for k in range(count):
             cut_layer(k, layer)
             if k == 0:
-                forward_corners(layer + 1, False)
+                forward_corners(layer + 1)
             ((re, im),) = hop([leave(k, layer)], phases[0], phases[1], pairs)
             waves[k, layer + 1, 0] = re
             waves[k, layer + 1, 1] = im
         return carry
 
-    forward_corners(0, False)
+    forward_corners(0)
     lax.fori_loop(0, last, onward, 0)
 
-    def record(k, layer, back_re, back_im):
-        wave_re, wave_im = waves[k, layer, 0], waves[k, layer, 1]
+    def record(k, layer, back_re, back_im, start, stop):
+        low, high = max(start - 1, 0), min(stop, width // 8)
+        rows, span = pl.ds(8 * low, 8 * (high - low)), slice(8 * low, 8 * high)
+        wave_re, wave_im = waves[k, layer, 0, rows, :], waves[k, layer, 1, rows, :]
+        back_re, back_im = back_re[span], back_im[span]
         shift = row_place(offsets[0, 0, k, 0], whole, width)[1]
         turn = lane_place(offsets[0, 0, k, 1])[1]
         terms = (wave_re * back_re + wave_im * back_im, wave_re * back_im - wave_im * back_re)
@@ -362,8 +363,17 @@
             blocks = jnp.stack([terms[c][:, j * LANES : j * LANES + LANES] for j in range(wide)])
             blocks = spread(blocks, turn, 2, LANES)
             for j in range(rounds):
-                part = spread(blocks[j].reshape(width // 8, 8, LANES), shift, 1, 8)
-                spans[k, c, j, pl.ds(pad // 8, width // 8 + 1)] = part
+                turned = pltpu.roll(blocks[j].reshape(high - low, 8, LANES), lax.rem(shift, 8), 1)
+                zero = jnp.zeros_like(turned[:1])
+                before, after = turned[: stop - 1 - low], turned[start - low :]
+                if start == 0:
+                    before = jnp.concatenate([zero, before], 0)
+                if stop > high:
+                    after = jnp.concatenate([after, zero], 0)
+                else:
+                    after = after[: stop - start]
+                moved = lax.broadcasted_iota(jnp.int32, before.shape, 1) < shift
+                spans[k, c, j, pl.ds(pad // 8 + start, stop - start)] = jnp.where(moved, before, after)
 
     def summed(c, block, start, size):
         found = None
@@ -375,12 +385,16 @@
             found = term if found is None else found + term
         return found.reshape(size, LANES)
 
-    def settle(layer):
-        def sums(start, size):
-            blocks = [[summed(c, j, start, size) for j in range(wide)] for c in range(2)]
-            outer_re, outer_im = (summed(c, wide, start, size) for c in range(2))
-            return blocks, (choose(outer_re, swapped(outer_im)), choose(swapped(outer_re), outer_im))
-
+    def sums(start, size):
+        blocks = [[summed(c, j, start, size) for j in range(wide)] for c in range(2)]
+        outer_re, outer_im = (summed(c, wide, start, size) for c in range(2))
+        return blocks, (choose(outer_re, swapped(outer_im)), choose(swapped(outer_re), outer_im))
+
+    def settle(layer, backs):
+        reach = HALO // 8
+        for k in range(count):
+            record(k, layer, *backs[k], 0, reach)
+            record(k, layer, *backs[k], width // 8 + 1 - reach, width // 8 + 1)
         for d, start in enumerate((0, HALO + tall)):
             blocks, outer = sums(start, HALO)
             for half, packs in enumerate((ends_of(blocks), middle_of(blocks))):
@@ -388,11 +402,12 @@
                     grow_out[layer, half, i, 1 - d] = packs[i]
             for side in range(2):
                 gcorner_out[layer, side, 1 - d] = outer[side]
+        for d in range(2):
+            grow_copy(layer, 1, d).start()
         for side in range(2):
             gcorner_copy(layer, side).start()
-        for d in range(2):
-            grow_copy(layer, 1, d).start()
-
+        for k in range(count):
+            record(k, layer, *backs[k], reach, width // 8 + 1 - reach)
         blocks, outer = sums(HALO, tall)
         for c in range(2):
             for j in range(wide):
@@ -400,6 +415,9 @@
         for side in range(2):
             gcol_out[layer, side] = outer[side]
             gcol_copy(layer, side).start()
+        for k in range(count):
+            for c in range(2):
+                waves[k, layer, c] = backs[k][c]
 
     def pass_on(layer):
         for side in range(2):
@@ -417,12 +435,7 @@
     far_re, far_im = forward(*(jnp.concatenate([v[c] for v in leaving], 1) for c in range(2)), pairs)
     misfit = far_re * far_re + far_im * far_im - ordered[...].reshape(far_re.shape)
     backs = inverse(misfit * far_re, misfit * far_im, pairs)
-    for k in range(count):
-        back_re, back_im = (v[:, k * width : (k + 1) * width] for v in backs)
-        record(k, last, back_re, back_im)
-        waves[k, last, 0] = back_re
-        waves[k, last, 1] = back_im
-    settle(last)
+    settle(last, [[v[:, k * width : (k + 1) * width] for v in backs] for k in range(count)])
 
     def backward(step, carry):
         layer = last - step
@@ -433,15 +446,21 @@
             fields.append(complex_product(back_re, back_im, slab_re, -slab_im))
         backs = hop(fields, phases[0], -phases[1], pairs)
         pass_on(layer)
-        for k, (re, im) in enumerate(backs):
-            record(k, layer - 1, re, im)
-            waves[k, layer - 1, 0] = re
-            waves[k, layer - 1, 1] = im
-        settle(layer - 1)
+        settle(layer - 1, backs)
         return carry
 
     lax.fori_loop(0, last, backward, 0)
     pass_on(0)
+    def close_in(layer, carry):
+        for d in range(2):
+            for half in range(2):
+                row_copy(layer, half, d).wait_send()
+            col_copy(layer, d).wait_send()
+            corner_copy(layer, d).wait_send()
+        return carry
+
+    lax.fori_loop(0, layers, close_in, 0)
+
     def finish(step, carry):
         layer = last - step
         for side in range(2):
@@ -471,18 +490,15 @@
 
     lax.fori_loop(0, layers, finish, 0)
 
-    def close(layer, carry):
+    def close_out(layer, carry):
         for d in range(2):
             for half in range(2):
-                row_copy(layer, half, d).wait_send()
                 grow_copy(layer, half, d).wait_send()
-            col_copy(layer, d).wait_send()
-            corner_copy(layer, d).wait_send()
             gcol_copy(layer, d).wait_send()
             gcorner_copy(layer, d).wait_send()
         return carry
 
-    lax.fori_loop(0, layers, close, 0)
+    lax.fori_loop(0, layers, close_out, 0)
 
 
 def publish_kernel(gradient, updated, gradient_out, updated_out, sems):

time: 65.1 us -> 64.7 us (level)
  no operation moved by 1% of the time
where the time goes in v4:
time: 64.7 us; the launch traced here: 64.6 us
  Pallas kernels  64 us (99%)
    pallas_call x1, Pallas kernels, on_device(): pl.pallas_call(step_kernel, out_shape=pair, in_specs=[anywhere] * 6, out_...  61.9 us
    pallas_call x1, Pallas kernels, on_device(): pl.pallas_call(publish_kernel, out_shape=[like, like], in_specs=[pl.Block...  2.07 us

profile of v4, /device:TPU:0, one launch (start us, length us, event | category | flops | bytes accessed | tf_op | source)
XLA Modules:
  0.0 64.6 jit_solution(17391611487980681305)
XLA Ops:
  0.6 61.9 %shard_map.77 = (f32[2,4,256,256]{3,2,1,0:T(8,128)S(1)}, f32[2,4,256,256]{3,2,1,0:T(8,128)S(1)}) custom-call(s32[1,1,2,2]{3,2,1,0:T(2,128)} %offsets_in.1, f32[2,4,256,256]{3,2,1,0:T(8,128)} %objects.1, f32[2,256,256]{2,1,0:T(8,128)} %bitcast.1, f32[2,256,256]{2,1,0:T(8,128)} %probe.1, f32[256,256]{1,0:T(8,128)} %propagator.1, ...), custom_call_target="tpu_custom_call" | custom-call | tf_op jit(solution)/shard_map/pallas_call | solution.py:527
  62.5 2.1 %shard_map.78 = (f32[2,4,256,256]{3,2,1,0:T(8,128)}, f32[2,4,256,256]{3,2,1,0:T(8,128)}) custom-call(f32[2,4,256,256]{3,2,1,0:T(8,128)S(1)} %get-tuple-element.4.gradient, f32[2,4,256,256]{3,2,1,0:T(8,128)S(1)} %get-tuple-element.5.updated), custom_call_target="tpu_custom_call" | custom-call | tf_op jit(solution)/shard_map/pallas_call | solution.py:554

commit v5 on v4

--- a/solution.py
+++ b/solution.py
@@ -250,6 +250,8 @@
             for half, packs in enumerate((ends_of(strip), middle_of(strip))):
                 for i in range(2):
                     row_out[layer, half, i, d] = packs[i]
+
+    def pack_sides(layer):
         head, tail = ends_of(lane_blocks(cells, layer, pl.ds(0, tall)))
         col_out[layer, 0] = tail
         col_out[layer, 1] = head
@@ -262,6 +264,7 @@
     def pack_and_launch(layer, carry):
         pack(layer)
         launch(layer)
+        pack_sides(layer)
         launch_sides(layer)
         return carry
 
@@ -272,6 +275,7 @@
     pack(0)
     pl.semaphore_wait(barrier, 4)
     launch(0)
+    pack_sides(0)
     launch_sides(0)
     for load in loads:
         load.start()
@@ -465,11 +469,12 @@
         layer = last - step
         for side in range(2):
             gcol_copy(layer, side).wait_recv()
-        for half in (1, 0):
-            for d in range(2):
-                grow_copy(layer, half, d).wait_recv()
-        spots = ((0, HALO, 0), (HALO, tall - 2 * HALO, None), (tall - HALO, HALO, 1))
+        spots = ((HALO, tall - 2 * HALO, None), (0, HALO, 0), (tall - HALO, HALO, 1))
         for start, size, d in spots:
+            if d == 0:
+                for half in (1, 0):
+                    for e in range(2):
+                        grow_copy(layer, half, e).wait_recv()
             rows = pl.ds(start, size)
             sums = lane_blocks(gradient, layer, rows)
             if d is not None:

time: 64.7 us -> 64.8 us (level)
  no operation moved by 1% of the time
where the time goes in v5:
time: 64.8 us; the launch traced here: 64.7 us
  Pallas kernels  64 us (99%)
    pallas_call x1, Pallas kernels, on_device(): pl.pallas_call(step_kernel, out_shape=pair, in_specs=[anywhere] * 6, out_...  62 us
    pallas_call x1, Pallas kernels, on_device(): pl.pallas_call(publish_kernel, out_shape=[like, like], in_specs=[pl.Block...  2.07 us

profile of v5, /device:TPU:0, one launch (start us, length us, event | category | flops | bytes accessed | tf_op | source)
XLA Modules:
  0.0 64.7 jit_solution(11148481369507191659)
XLA Ops:
  0.6 62.0 %shard_map.77 = (f32[2,4,256,256]{3,2,1,0:T(8,128)S(1)}, f32[2,4,256,256]{3,2,1,0:T(8,128)S(1)}) custom-call(s32[1,1,2,2]{3,2,1,0:T(2,128)} %offsets_in.1, f32[2,4,256,256]{3,2,1,0:T(8,128)} %objects.1, f32[2,256,256]{2,1,0:T(8,128)} %bitcast.1, f32[2,256,256]{2,1,0:T(8,128)} %probe.1, f32[256,256]{1,0:T(8,128)} %propagator.1, ...), custom_call_target="tpu_custom_call" | custom-call | tf_op jit(solution)/shard_map/pallas_call | solution.py:532
  62.6 2.1 %shard_map.78 = (f32[2,4,256,256]{3,2,1,0:T(8,128)}, f32[2,4,256,256]{3,2,1,0:T(8,128)}) custom-call(f32[2,4,256,256]{3,2,1,0:T(8,128)S(1)} %get-tuple-element.4.gradient, f32[2,4,256,256]{3,2,1,0:T(8,128)S(1)} %get-tuple-element.5.updated), custom_call_target="tpu_custom_call" | custom-call | tf_op jit(solution)/shard_map/pallas_call | solution.py:559
